TPU v7x, 32 devices: a whole 2x2x4 slice. The times are simulated.
32 devices in a mesh: space: 8 (over z, y), species: 4 (over x, core).
Axes of the slice: x: 2, y: 2, z: 4, core: 2. Of those that a mesh axis runs over, the one named last changes fastest.
Arguments:
- effects: float32 [48, 256, 2048], P('space', None, 'species'), may hold values from -1.2 to 1.2
- kappa_sq: float32 [48, 256], P('space'), may hold values from 0.1 to 2
- growth: float32 [48, 256, 128], P('space'), may hold values from -6 to 6
- tree_species: int32 [48, 256, 128], P('space'), may hold values from 0 to 2047
- tree_counts: int32 [48, 256], P('space'), may hold values from 1 to 128, as said below
- noise_precision: float32 [2048], P('species'), may hold values from 0.5 to 4
- species_precision: bfloat16 [2048, 2048], P(None, 'species'), as said below
Outputs:
- grad_effects: float32 [48, 256, 2048], P('space', None, 'species')
- gram: float32 [2048, 2048], P('space', 'species')
Inputs may be any that keep to these rules, and one draw needn't show every extreme that they name: `tree_counts`: some plot has 128 live trees. species_precision is symmetric.
All inputs are finite; a program needn't handle non-finite values.
Results may differ from a plain program's by a relative error of at most 0.0029.
Values may be sent and summed in bfloat16 or wider, within the bound.
No kernel may reach another device: no remote copies, remote signals or barrier semaphores. Data moves between devices by JAX's collectives and lax.ppermute only.
A program may use at most 128 MiB of HBM per device.

v0:
```python
import math

import jax
import jax.numpy as jnp
from jax import lax
from jax.sharding import PartitionSpec as P


def with_halo(block, sides, width):
    for axis, dim in sides:
        count = lax.axis_size(axis)
        forward = [(i, i + 1) for i in range(count - 1)]
        backward = [(target, source) for source, target in forward]
        low = lax.ppermute(
            lax.slice_in_dim(block, block.shape[dim] - width, None, axis=dim), axis, forward
        )
        high = lax.ppermute(lax.slice_in_dim(block, 0, width, axis=dim), axis, backward)
        block = jnp.concatenate([low, block, high], axis=dim)
    return block


def local_k(extended, kappa_rim):
    padded = jnp.pad(extended, ((0, 0), (1, 1), (0, 0)))
    centre_cells = extended[1:-1]
    beside = extended[2:] + extended[:-2] + padded[1:-1, 2:] + padded[1:-1, :-2]
    return (kappa_rim[..., None] + 4.0) * centre_cells - beside


def shards(
    effects, kappa_sq, growth, tree_species, tree_counts, noise_precision, species_precision
):
    grid_rows, grid_cols, columns = effects.shape
    space_count = lax.axis_size("space")
    first_column = lax.axis_index("species") * columns
    plot_count = grid_rows * grid_cols
    extended, kappa_wide = (
        with_halo(effects, (("space", 0),), 1),
        with_halo(kappa_sq, (("space", 0),), 1),
    )
    first_pass = local_k(extended, kappa_wide[1:-1])
    first_wide = with_halo(first_pass, (("space", 0),), 1)
    spatial = local_k(first_wide, kappa_wide[1:-1])
    spatial_low = spatial.astype(jnp.bfloat16).reshape(plot_count, columns)
    effects_low = effects.astype(jnp.bfloat16).reshape(plot_count, columns)
    effect_piece = lax.all_gather(effects_low, "species", axis=1, tiled=True)
    spatial_piece = lax.all_gather(spatial_low, "species", axis=1, tiled=True)
    prior_part = jnp.dot(spatial_piece, species_precision, preferred_element_type=jnp.float32)
    block_term = lax.dot_general(
        effect_piece, spatial_low, (((0,), (0,)), ((), ())), preferred_element_type=jnp.float32
    )
    gram_scale = -0.5 / (plot_count * space_count)
    gram = lax.psum_scatter(block_term * gram_scale, "space", scatter_dimension=0, tiled=True)
    tree_slots = growth.shape[2]
    live_tree = lax.broadcasted_iota(jnp.int32, growth.shape, 2) < tree_counts[..., None]
    local_column = (tree_species - first_column).reshape(plot_count, tree_slots)
    live_flat = live_tree.reshape(plot_count, tree_slots)
    growth_flat = growth.astype(jnp.bfloat16).reshape(plot_count, tree_slots)
    block_plots = math.gcd(plot_count, 128)
    block_count = plot_count // block_plots
    stacked_values = jnp.stack([growth_flat, jnp.ones_like(growth_flat)], axis=2)

    def block_sums(operands):
        column_block, live_block, value_block = operands
        column_iota = lax.broadcasted_iota(jnp.int32, (1, 1, columns), 2)
        one_hot = ((column_block[..., None] == column_iota) & live_block[..., None]).astype(
            jnp.bfloat16
        )
        return jnp.einsum("ptc,ptk->pkc", one_hot, value_block, preferred_element_type=jnp.float32)

    summed = lax.map(
        block_sums,
        (
            local_column.reshape(block_count, block_plots, tree_slots),
            live_flat.reshape(block_count, block_plots, tree_slots),
            stacked_values.reshape(block_count, block_plots, tree_slots, 2),
        ),
    )
    summed = summed.reshape(plot_count, 2, columns)
    growth_sum = summed[:, 0]
    tally = summed[:, 1]
    grad_flat = (
        noise_precision[None, :] * (growth_sum - tally * effects.reshape(plot_count, columns))
        - prior_part
    )
    return (grad_flat.reshape(grid_rows, grid_cols, columns), gram)


def solution(mesh):
    return jax.shard_map(
        shards,
        mesh=mesh,
        in_specs=(
            P("space", None, "species"),
            P("space", None),
            P("space", None, None),
            P("space", None, None),
            P("space", None),
            P("species"),
            P(None, "species"),
        ),
        out_specs=(P("space", None, "species"), P("space", "species")),
        check_vma=False,
    )
```

profile of v0, /device:TPU:0, one launch (start us, length us, event | category | flops | bytes accessed | tf_op | source)
XLA Modules:
  0.0 239.3 jit_solution(775646641542731349)
XLA Ops:
  7.2 1.4 fusion.22
  8.6 4.9 %collective-permute-start.1 = (f32[1,256,512]{2,1,0:T(8,128)S(1)}, f32[1,256,512]{2,1,0:T(8,128)S(1)}, u32[]{:S(2)}, u32[]{:S(2)}) collective-permute-start(f32[1,256,512]{2,1,0:T(8,128)S(1)} %get-tuple-element.46), channel_id=1, source_target_pairs={{0,4},{4,8},{8,12},{12,16},{16,20},{20,24},{24,28},{1,5},{5,9},{9,... | collective-permute-start | bytes 1572872 | tf_op jit(solution)/shard_map/ppermute | solution.py:14
  13.6 1.3 collective-permute-start
  14.9 0.7 broadcast_add_fusion
  15.6 20.4 %collective-permute-done.1 = f32[1,256,512]{2,1,0:T(8,128)S(1)} collective-permute-done((f32[1,256,512]{2,1,0:T(8,128)S(1)}, f32[1,256,512]{2,1,0:T(8,128)S(1)}, u32[]{:S(2)}, u32[]{:S(2)}) %collective-permute-start.1) | collective-permute-done | bytes 524320 | tf_op jit(solution)/shard_map/ppermute | solution.py:14
  35.9 2.5 %select_maximum_fusion.2 = f32[8,258,512]{2,1,0:T(8,128)S(1)} fusion(f32[1,256,512]{2,1,0:T(8,128)S(1)} %collective-permute-done, f32[6,256,512]{2,1,0:T(8,128)} %param.9, f32[1,256,512]{2,1,0:T(8,128)S(1)} %collective-permute-done.1), kind=kLoop, calls=%fused_computation.16 | loop fusion | flops 8454144 | bytes 8421376 | tf_op jit(solution)/shard_map/concatenate | solution.py:18
  38.5 2.7 %fusion.20 = (bf16[6,256,512]{2,1,0:T(8,128)(2,1)}, f32[6,256,512]{2,1,0:T(8,128)}) fusion(f32[6,256,512]{2,1,0:T(8,128)S(1)} %copy-done.2, f32[8,258,512]{2,1,0:T(8,128)S(1)} %select_maximum_fusion.2, f32[1,256,512]{2,1,0:T(8,128)S(1)} %collective-permute-done.1, f32[1,256,512]{2,1,0:T(8,128)S(1)} %collective-permute-done, f32[6,256]{1,0:T(8,128)S(1)} %broadcast_add_fusion), kind=kLoop, calls=%fused_computation.42 | loop fusion | flops 6291456 | bytes 15210496 | tf_op jit(solution)/shard_map/convert_element_type | solution.py:44
  41.2 1.3 fusion.21
  42.5 4.4 %collective-permute-start.3 = (f32[1,256,512]{2,1,0:T(8,128)S(1)}, f32[1,256,512]{2,1,0:T(8,128)S(1)}, u32[]{:S(2)}, u32[]{:S(2)}) collective-permute-start(f32[1,256,512]{2,1,0:T(8,128)S(1)} %get-tuple-element.44), channel_id=1, source_target_pairs={{0,4},{4,8},{8,12},{12,16},{16,20},{20,24},{24,28},{1,5},{5,9},{9,... | collective-permute-start | bytes 1572872 | tf_op jit(solution)/shard_map/ppermute | solution.py:14
  46.9 1.6 collective-permute-start.2
  48.5 19.9 %collective-permute-done.3 = f32[1,256,512]{2,1,0:T(8,128)S(1)} collective-permute-done((f32[1,256,512]{2,1,0:T(8,128)S(1)}, f32[1,256,512]{2,1,0:T(8,128)S(1)}, u32[]{:S(2)}, u32[]{:S(2)}) %collective-permute-start.3) | collective-permute-done | bytes 524320 | tf_op jit(solution)/shard_map/ppermute | solution.py:14
  68.4 2.5 %select_maximum_fusion = f32[8,258,512]{2,1,0:T(8,128)S(1)} fusion(f32[1,256,512]{2,1,0:T(8,128)S(1)} %collective-permute-done.2, f32[6,256,512]{2,1,0:T(8,128)} %get-tuple-element.43, f32[1,256,512]{2,1,0:T(8,128)S(1)} %collective-permute-done.3), kind=kLoop, calls=%fused_computation.14 | loop fusion | flops 8454144 | bytes 8421376 | tf_op jit(solution)/shard_map/concatenate | solution.py:18
  71.0 1.7 fusion.13
  72.7 0.2 reduce-scatter.2.cloned.1.call-start
  73.1 6.1 %copy.9 = bf16[1536,128,1]{1,2,0:T(2,128)(2,1)S(1)} copy(bf16[1536,128,1]{1,0,2:T(8,128)(2,1)S(1)} %bitcast.50) | data formatting | bytes 786432 | tf_op jit(solution)/shard_map/stack;reshape | solution.py:60
  79.2 1.6 stack.3
  80.8 0.3 iota_compare_fusion.3
  81.1 1.2 broadcast_subtract_fusion
  82.3 7.5 %all-gather.5.cloned.1.call-done = bf16[1536,2048]{1,0:T(8,128)(2,1)} async-done(((bf16[1536,512]{1,0:T(8,128)(2,1)}), bf16[1536,2048]{1,0:T(8,128)(2,1)}) %all-gather.5.cloned.1.call-update) | async-done | bytes 6291472 | tf_op jit(solution)/shard_map/all_gather | solution.py:45
  89.8 8.8 %multiply_bitcast_fusion = f32[2048,512]{0,1:T(8,128)} fusion(bf16[1536,512]{1,0:T(8,128)(2,1)} %bitcast.47, bf16[1536,2048]{1,0:T(8,128)(2,1)} %all-gather.5.cloned.1.call-done), kind=kOutput, calls=%fused_computation.19 | convolution fusion | flops 3222274048 | bytes 12058624 | tf_op jit(solution)/shard_map/dot_general | solution.py:48
  98.7 109.4 %while.10 = (s32[]{:T(128)}, f32[12,128,2,512]{3,1,0,2:T(8,128)}, bf16[12,128,128,2]{2,3,1,0:T(2,128)(2,1)}, s32[12,128,128]{2,1,0:T(8,128)S(1)}, pred[12,128,128]{2,1,0:T(8,128)(4,1)S(1)}, /*index=5*/s32[]{:T(128)}) while((s32[]{:T(128)}, f32[12,128,2,512]{3,1,0,2:T(8,128)}, bf16[12,128,128,2]{2,3,1,0:T(2,128)(2,1)}, ...), condition=%wide.region_1.2_spmd, body=%wide.region_0.1_spmd.sunk | while | flops 50331648 | bytes 1884253 | solution.py:70
  98.7 8.2 %fusion.32 = f32[1,128,2,512]{3,2,1,0:T(2,128)S(1)} fusion(s32[128,128]{1,0:T(8,128)S(1)} %dynamic-slice_bitcast_fusion.4, pred[128,128]{1,0:T(8,128)(4,1)S(1)} %dynamic-slice_bitcast_fusion.5, bf16[12,128,128,2]{2,3,1,0:T(2,128)(2,1)} %get-tuple-element.93, s32[]{:T(128)S(6)} %copy.22), kind=kOutput, calls=%fused_computation.5.clone.1 | convolution fusion | flops 50331648 | bytes 671748 | tf_op jit(solution)/shard_map/while/body/eval_jaxpr/ptc,ptk->pkc/dot_general | solution.py:68
  106.9 0.9 copy_dynamic-update-slice_fusion.2
  107.8 8.2 %fusion.32 = f32[1,128,2,512]{3,2,1,0:T(2,128)S(1)} fusion(s32[128,128]{1,0:T(8,128)S(1)} %dynamic-slice_bitcast_fusion.4, pred[128,128]{1,0:T(8,128)(4,1)S(1)} %dynamic-slice_bitcast_fusion.5, bf16[12,128,128,2]{2,3,1,0:T(2,128)(2,1)} %get-tuple-element.93, s32[]{:T(128)S(6)} %copy.22), kind=kOutput, calls=%fused_computation.5.clone.1 | convolution fusion | flops 50331648 | bytes 671748 | tf_op jit(solution)/shard_map/while/body/eval_jaxpr/ptc,ptk->pkc/dot_general | solution.py:68
  116.0 0.9 copy_dynamic-update-slice_fusion.2
  116.9 8.2 %fusion.32 = f32[1,128,2,512]{3,2,1,0:T(2,128)S(1)} fusion(s32[128,128]{1,0:T(8,128)S(1)} %dynamic-slice_bitcast_fusion.4, pred[128,128]{1,0:T(8,128)(4,1)S(1)} %dynamic-slice_bitcast_fusion.5, bf16[12,128,128,2]{2,3,1,0:T(2,128)(2,1)} %get-tuple-element.93, s32[]{:T(128)S(6)} %copy.22), kind=kOutput, calls=%fused_computation.5.clone.1 | convolution fusion | flops 50331648 | bytes 671748 | tf_op jit(solution)/shard_map/while/body/eval_jaxpr/ptc,ptk->pkc/dot_general | solution.py:68
  125.1 0.9 copy_dynamic-update-slice_fusion.2
  126.1 8.2 %fusion.32 = f32[1,128,2,512]{3,2,1,0:T(2,128)S(1)} fusion(s32[128,128]{1,0:T(8,128)S(1)} %dynamic-slice_bitcast_fusion.4, pred[128,128]{1,0:T(8,128)(4,1)S(1)} %dynamic-slice_bitcast_fusion.5, bf16[12,128,128,2]{2,3,1,0:T(2,128)(2,1)} %get-tuple-element.93, s32[]{:T(128)S(6)} %copy.22), kind=kOutput, calls=%fused_computation.5.clone.1 | convolution fusion | flops 50331648 | bytes 671748 | tf_op jit(solution)/shard_map/while/body/eval_jaxpr/ptc,ptk->pkc/dot_general | solution.py:68
  134.3 0.9 copy_dynamic-update-slice_fusion.2
  135.2 8.2 %fusion.32 = f32[1,128,2,512]{3,2,1,0:T(2,128)S(1)} fusion(s32[128,128]{1,0:T(8,128)S(1)} %dynamic-slice_bitcast_fusion.4, pred[128,128]{1,0:T(8,128)(4,1)S(1)} %dynamic-slice_bitcast_fusion.5, bf16[12,128,128,2]{2,3,1,0:T(2,128)(2,1)} %get-tuple-element.93, s32[]{:T(128)S(6)} %copy.22), kind=kOutput, calls=%fused_computation.5.clone.1 | convolution fusion | flops 50331648 | bytes 671748 | tf_op jit(solution)/shard_map/while/body/eval_jaxpr/ptc,ptk->pkc/dot_general | solution.py:68
  143.4 0.9 copy_dynamic-update-slice_fusion.2
  144.3 8.2 %fusion.32 = f32[1,128,2,512]{3,2,1,0:T(2,128)S(1)} fusion(s32[128,128]{1,0:T(8,128)S(1)} %dynamic-slice_bitcast_fusion.4, pred[128,128]{1,0:T(8,128)(4,1)S(1)} %dynamic-slice_bitcast_fusion.5, bf16[12,128,128,2]{2,3,1,0:T(2,128)(2,1)} %get-tuple-element.93, s32[]{:T(128)S(6)} %copy.22), kind=kOutput, calls=%fused_computation.5.clone.1 | convolution fusion | flops 50331648 | bytes 671748 | tf_op jit(solution)/shard_map/while/body/eval_jaxpr/ptc,ptk->pkc/dot_general | solution.py:68
  152.5 0.9 copy_dynamic-update-slice_fusion.2
  153.4 8.2 %fusion.32 = f32[1,128,2,512]{3,2,1,0:T(2,128)S(1)} fusion(s32[128,128]{1,0:T(8,128)S(1)} %dynamic-slice_bitcast_fusion.4, pred[128,128]{1,0:T(8,128)(4,1)S(1)} %dynamic-slice_bitcast_fusion.5, bf16[12,128,128,2]{2,3,1,0:T(2,128)(2,1)} %get-tuple-element.93, s32[]{:T(128)S(6)} %copy.22), kind=kOutput, calls=%fused_computation.5.clone.1 | convolution fusion | flops 50331648 | bytes 671748 | tf_op jit(solution)/shard_map/while/body/eval_jaxpr/ptc,ptk->pkc/dot_general | solution.py:68
  161.6 0.9 copy_dynamic-update-slice_fusion.2
  162.6 8.2 %fusion.32 = f32[1,128,2,512]{3,2,1,0:T(2,128)S(1)} fusion(s32[128,128]{1,0:T(8,128)S(1)} %dynamic-slice_bitcast_fusion.4, pred[128,128]{1,0:T(8,128)(4,1)S(1)} %dynamic-slice_bitcast_fusion.5, bf16[12,128,128,2]{2,3,1,0:T(2,128)(2,1)} %get-tuple-element.93, s32[]{:T(128)S(6)} %copy.22), kind=kOutput, calls=%fused_computation.5.clone.1 | convolution fusion | flops 50331648 | bytes 671748 | tf_op jit(solution)/shard_map/while/body/eval_jaxpr/ptc,ptk->pkc/dot_general | solution.py:68
  170.7 0.9 copy_dynamic-update-slice_fusion.2
  171.7 8.2 %fusion.32 = f32[1,128,2,512]{3,2,1,0:T(2,128)S(1)} fusion(s32[128,128]{1,0:T(8,128)S(1)} %dynamic-slice_bitcast_fusion.4, pred[128,128]{1,0:T(8,128)(4,1)S(1)} %dynamic-slice_bitcast_fusion.5, bf16[12,128,128,2]{2,3,1,0:T(2,128)(2,1)} %get-tuple-element.93, s32[]{:T(128)S(6)} %copy.22), kind=kOutput, calls=%fused_computation.5.clone.1 | convolution fusion | flops 50331648 | bytes 671748 | tf_op jit(solution)/shard_map/while/body/eval_jaxpr/ptc,ptk->pkc/dot_general | solution.py:68
  179.9 0.9 copy_dynamic-update-slice_fusion.2
  180.8 8.2 %fusion.32 = f32[1,128,2,512]{3,2,1,0:T(2,128)S(1)} fusion(s32[128,128]{1,0:T(8,128)S(1)} %dynamic-slice_bitcast_fusion.4, pred[128,128]{1,0:T(8,128)(4,1)S(1)} %dynamic-slice_bitcast_fusion.5, bf16[12,128,128,2]{2,3,1,0:T(2,128)(2,1)} %get-tuple-element.93, s32[]{:T(128)S(6)} %copy.22), kind=kOutput, calls=%fused_computation.5.clone.1 | convolution fusion | flops 50331648 | bytes 671748 | tf_op jit(solution)/shard_map/while/body/eval_jaxpr/ptc,ptk->pkc/dot_general | solution.py:68
  189.0 0.9 copy_dynamic-update-slice_fusion.2
  189.9 8.2 %fusion.32 = f32[1,128,2,512]{3,2,1,0:T(2,128)S(1)} fusion(s32[128,128]{1,0:T(8,128)S(1)} %dynamic-slice_bitcast_fusion.4, pred[128,128]{1,0:T(8,128)(4,1)S(1)} %dynamic-slice_bitcast_fusion.5, bf16[12,128,128,2]{2,3,1,0:T(2,128)(2,1)} %get-tuple-element.93, s32[]{:T(128)S(6)} %copy.22), kind=kOutput, calls=%fused_computation.5.clone.1 | convolution fusion | flops 50331648 | bytes 671748 | tf_op jit(solution)/shard_map/while/body/eval_jaxpr/ptc,ptk->pkc/dot_general | solution.py:68
  198.1 0.9 copy_dynamic-update-slice_fusion.2
  199.0 8.2 %fusion.32 = f32[1,128,2,512]{3,2,1,0:T(2,128)S(1)} fusion(s32[128,128]{1,0:T(8,128)S(1)} %dynamic-slice_bitcast_fusion.4, pred[128,128]{1,0:T(8,128)(4,1)S(1)} %dynamic-slice_bitcast_fusion.5, bf16[12,128,128,2]{2,3,1,0:T(2,128)(2,1)} %get-tuple-element.93, s32[]{:T(128)S(6)} %copy.22), kind=kOutput, calls=%fused_computation.5.clone.1 | convolution fusion | flops 50331648 | bytes 671748 | tf_op jit(solution)/shard_map/while/body/eval_jaxpr/ptc,ptk->pkc/dot_general | solution.py:68
  207.2 0.9 copy_dynamic-update-slice_fusion.2
  208.1 10.2 %convolution_subtract_fusion = f32[1536,512]{1,0:T(8,128)} fusion(bf16[1536,2048]{1,0:T(8,128)(2,1)} %all-gather.3.cloned.1.call-done, bf16[2048,512]{1,0:T(8,128)(2,1)S(1)} %copy-done, f32[1536,512]{1,0:T(8,128)} %bitcast.45, f32[1536,2,512]{2,0,1:T(8,128)} %bitcast.52, f32[512]{0:T(512)S(1)} %copy-done.5), kind=kOutput, calls=%fused_computation.20 | convolution fusion | flops 3224371200 | bytes 20973568 | tf_op jit(solution)/shard_map/dot_general | solution.py:47
  218.2 12.5 %reduce-scatter.2.cloned.1.call-done = f32[256,512]{0,1:T(8,128)} async-done(((f32[2048,512]{0,1:T(8,128)}), f32[256,512]{0,1:T(8,128)}) %reduce-scatter.2.cloned.1.call-update) | async-done | bytes 524304 | tf_op jit(solution)/shard_map/reduce_scatter | solution.py:52
  230.7 2.0 copy.11
  (47 shorter events, 0.3 us)
Async XLA Ops:
  7.2 200.9 %copy-start = (bf16[2048,512]{1,0:T(8,128)(2,1)S(1)}, bf16[2048,512]{1,0:T(8,128)(2,1)}, u32[]{:S(2)}) copy-start(bf16[2048,512]{1,0:T(8,128)(2,1)} %param.15) | copy-start | bytes 6291460
  7.2 82.7 %all-gather.5.cloned.1.call-start = ((), (), s32[]{:S(2)}) async-start(), calls=%async_computation.2 | async-start | bytes 7864320 | tf_op jit(solution)/shard_map/all_gather | solution.py:45
  8.6 27.3 %collective-permute-start.1 = (f32[1,256,512]{2,1,0:T(8,128)S(1)}, f32[1,256,512]{2,1,0:T(8,128)S(1)}, u32[]{:S(2)}, u32[]{:S(2)}) collective-permute-start(f32[1,256,512]{2,1,0:T(8,128)S(1)} %get-tuple-element.46), channel_id=1, source_target_pairs={{0,4},{4,8},{8,12},{12,16},{16,20},{20,24},{24,28},{1,5},{5,9},{9,... | collective-permute-start | bytes 1572872 | tf_op jit(solution)/shard_map/ppermute | solution.py:14
  13.6 22.4 %collective-permute-start = (f32[1,256,512]{2,1,0:T(8,128)S(1)}, f32[1,256,512]{2,1,0:T(8,128)S(1)}, u32[]{:S(2)}, u32[]{:S(2)}) collective-permute-start(f32[1,256,512]{2,1,0:T(8,128)S(1)} %get-tuple-element.47), channel_id=1, source_target_pairs={{4,0},{8,4},{12,8},{16,12},{20,16},{24,20},{28,24},{5,1},{9,5},{13... | collective-permute-start | bytes 1572872 | tf_op jit(solution)/shard_map/ppermute | solution.py:17
  15.6 22.9 %copy-start.2 = (f32[6,256,512]{2,1,0:T(8,128)S(1)}, f32[6,256,512]{2,1,0:T(8,128)}, u32[]{:S(2)}) copy-start(f32[6,256,512]{2,1,0:T(8,128)} %param.9) | copy-start | bytes 9437188
  41.2 166.9 %all-gather.3.cloned.1.call-start = ((), (), s32[]{:S(2)}) async-start(), calls=%async_computation.1 | async-start | bytes 7864320 | tf_op jit(solution)/shard_map/all_gather | solution.py:46
  42.5 25.9 %collective-permute-start.3 = (f32[1,256,512]{2,1,0:T(8,128)S(1)}, f32[1,256,512]{2,1,0:T(8,128)S(1)}, u32[]{:S(2)}, u32[]{:S(2)}) collective-permute-start(f32[1,256,512]{2,1,0:T(8,128)S(1)} %get-tuple-element.44), channel_id=1, source_target_pairs={{0,4},{4,8},{8,12},{12,16},{16,20},{20,24},{24,28},{1,5},{5,9},{9,... | collective-permute-start | bytes 1572872 | tf_op jit(solution)/shard_map/ppermute | solution.py:14
  46.9 24.0 %copy-start.1 = (f32[6,256,512]{2,1,0:T(8,128)S(1)}, f32[6,256,512]{2,1,0:T(8,128)}, u32[]{:S(2)}) copy-start(f32[6,256,512]{2,1,0:T(8,128)} %get-tuple-element.43) | copy-start | bytes 9437188
  46.9 21.5 %collective-permute-start.2 = (f32[1,256,512]{2,1,0:T(8,128)S(1)}, f32[1,256,512]{2,1,0:T(8,128)S(1)}, u32[]{:S(2)}, u32[]{:S(2)}) collective-permute-start(f32[1,256,512]{2,1,0:T(8,128)S(1)} %get-tuple-element.45), channel_id=1, source_target_pairs={{4,0},{8,4},{12,8},{16,12},{20,16},{24,20},{28,24},{5,1},{9,5},{13... | collective-permute-start | bytes 1572872 | tf_op jit(solution)/shard_map/ppermute | solution.py:17
  71.0 2.0 copy-start.4
  71.0 2.0 copy-start.3
  72.7 158.0 %reduce-scatter.2.cloned.1.call-start = ((), (), s32[]{:S(2)}) async-start(), calls=%async_computation.3 | async-start | bytes 4718592 | tf_op jit(solution)/shard_map/reduce_scatter | solution.py:52
  98.6 109.4 %copy-start.5 = (f32[512]{0:T(512)S(1)}, f32[512]{0:T(512)}, u32[]{:S(2)}) copy-start(f32[512]{0:T(512)} %param.14) | copy-start | bytes 6148
Sparse Core Ops, SparseCore 0:
  41.3 48.4 all-gather.4
  92.0 46.3 all-gather.2
  142.0 88.6 reduce-scatter.1
where the time goes:
time: 240 us; the launch traced here: 239 us
  matrix products  117 us (49%)
  waiting for transfers between devices  60.3 us (25%)
  local copies, waits for them, and re-layouts  23.5 us (10%)
  between operations  13.9 us (6%)
  starting transfers between devices  12.5 us (5%)
  other arithmetic  11.6 us (5%)
    dot_general x12, matrix products, block_sums(): jnp.einsum('ptc,ptk->pkc', one_hot, value_block, preferred_element_type=j...  98.3 us
    ppermute x2, waiting for transfers between devices, with_halo(): lax.ppermute(lax.slice_in_dim(block, block.shape[dim] - width, None, axis...  40.3 us
    reduce_scatter x1, waiting for transfers between devices, shards(): lax.psum_scatter(block_term * gram_scale, 'space', scatter_dimension=0, t...  12.5 us
    dynamic_update_slice x12, local copies, waits for them, and re-layouts, shards(): lax.map(block_sums, (local_column.reshape(block_count, block_plots, tree_...  10.9 us
    dot_general x1, matrix products, shards(): jnp.dot(spatial_piece, species_precision, preferred_element_type=jnp.floa...  10.2 us
    ppermute x2, starting transfers between devices, with_halo(): lax.ppermute(lax.slice_in_dim(block, block.shape[dim] - width, None, axis...  9.35 us
    dot_general x1, matrix products, shards(): lax.dot_general(effect_piece, spatial_low, (((0,), (0,)), ((), ())), pref...  8.78 us
    another operation x2, local copies, waits for them, and re-layouts, shards(): jnp.stack([growth_flat, jnp.ones_like(growth_flat)], axis=2)  7.74 us
  transfers between devices with their start and end apart: 7, of which 4 were waited for; matrix products, arithmetic and copies ran while one was open for 60% of the time, Pallas kernels for 0%

commit v1 on v0

v1 whole, which is shorter than its diff:
```python
import functools

import jax
import jax.numpy as jnp
from jax import lax
from jax.experimental import pallas as pl
from jax.experimental.pallas import tpu as pltpu
from jax.sharding import PartitionSpec as P


LANES = 128


def xor_swap(value, axis, mask):
    count = lax.axis_size(axis)
    return lax.ppermute(value, axis, [(i, i ^ mask) for i in range(count)])


def tree_kernel(groups, first_ref, effects_ref, growth_ref, species_ref, counts_ref, noise_ref, *rest):
    out_ref = rest[-1]
    rows, slots = growth_ref.shape
    bits = LANES.bit_length() - 1
    codes = groups * 8
    low_iota = lax.broadcasted_iota(jnp.int32, (LANES, slots), 0).astype(jnp.bfloat16)
    code_iota = lax.broadcasted_iota(jnp.int32, (codes, slots), 0).astype(jnp.bfloat16)
    slot_iota = lax.broadcasted_iota(jnp.int32, (8, slots), 1)
    row_iota = lax.broadcasted_iota(jnp.int32, (8, slots), 0)
    one, zero = jnp.bfloat16(1.0), jnp.bfloat16(0.0)
    first_column = first_ref[0]

    def step(index, carry):
        at = pl.ds(pl.multiple_of(index * 8, 8), 8)
        local = species_ref[at, :] - first_column
        group = local >> bits
        valid = (slot_iota < counts_ref[at, :]) & (group >= 0) & (group < groups)
        code = jnp.where(valid, group * 8 + row_iota, -1).astype(jnp.float32)
        low = (local & (LANES - 1)).astype(jnp.float32)
        value = growth_ref[at, :].astype(jnp.bfloat16).astype(jnp.float32)
        lefts, rights = [], []
        for plot in range(8):
            low_row = jnp.broadcast_to(low[plot : plot + 1], (LANES, slots)).astype(jnp.bfloat16)
            code_row = jnp.broadcast_to(code[plot : plot + 1], (codes, slots)).astype(jnp.bfloat16)
            value_row = jnp.broadcast_to(value[plot : plot + 1], (codes, slots)).astype(jnp.bfloat16)
            match = code_row == code_iota
            rights.append(jnp.where(low_row == low_iota, one, zero))
            lefts.append(
                jnp.concatenate([jnp.where(match, value_row, zero), jnp.where(match, one, zero)], axis=0)
            )
        sums = lax.dot_general(
            jnp.concatenate(lefts, axis=1),
            jnp.concatenate(rights, axis=1),
            (((1,), (1,)), ((), ())),
            preferred_element_type=jnp.float32,
        )
        for group_at in range(groups):
            cols = pl.ds(group_at * LANES, LANES)
            growth_sum = sums[group_at * 8 : group_at * 8 + 8]
            tally = sums[codes + group_at * 8 : codes + group_at * 8 + 8]
            out_ref[at, cols] = noise_ref[:, cols] * (growth_sum - tally * effects_ref[at, cols])
        return carry

    lax.fori_loop(0, rows // 8, step, 0, unroll=16)


def tree_term(effects, growth, species, counts, noise, first_column, start, length, before):
    plots, columns = effects.shape
    slots = growth.shape[1]
    block = 128
    first = start // block
    row = lambda width: pl.BlockSpec((block, width), lambda i: (first + i, 0))
    held = [] if before is None else [before]
    return pl.pallas_call(
        functools.partial(tree_kernel, columns // LANES),
        grid=(length // block,),
        in_specs=[
            pl.BlockSpec(memory_space=pltpu.SMEM),
            row(columns),
            row(slots),
            row(slots),
            row(1),
            pl.BlockSpec((1, columns), lambda i: (0, 0)),
        ]
        + [pl.BlockSpec(memory_space=pl.ANY)] * len(held),
        out_specs=row(columns),
        out_shape=jax.ShapeDtypeStruct((plots, columns), jnp.float32),
        input_output_aliases={6: 0} if held else {},
        cost_estimate=pl.CostEstimate(
            flops=2 * length * slots * 64 * 128, bytes_accessed=8 * length * (slots + columns), transcendentals=0
        ),
        name="tree_term",
    )(first_column.reshape(1), effects, growth, species, counts.reshape(plots, 1), noise.reshape(1, columns), *held)


def k_row(above, centre, below, kappa):
    at = lax.broadcasted_iota(jnp.int32, centre.shape, 0)
    last = centre.shape[0] - 1
    left = jnp.where(at == 0, 0.0, pltpu.roll(centre, 1, axis=0))
    right = jnp.where(at == last, 0.0, pltpu.roll(centre, last, axis=0))
    return (kappa + 4.0) * centre - (below + above + right + left)


def mid_kernel(rows, with_wide, *refs):
    if with_wide:
        x_ref, kappa_ref, low_ref, wide_ref = refs
        get = lambda r: x_ref[r]
    else:
        x_ref, top_ref, bottom_ref, kappa_ref, low_ref = refs
        get = lambda r: top_ref[0] if r == 0 else bottom_ref[0] if r == rows - 1 else x_ref[r - 1]
    for r in range(1, rows - 1):
        value = k_row(get(r - 1), get(r), get(r + 1), kappa_ref[r])
        low_ref[r - 1] = value.astype(low_ref.dtype)
        if with_wide:
            wide_ref[r - 1] = value


def edge_kernel(with_wide, above_ref, first_ref, second_ref, before_ref, last_ref, below_ref, kappa_ref, *outs):
    rows = kappa_ref.shape[0]
    top = k_row(above_ref[0], first_ref[0], second_ref[0], kappa_ref[0])
    bottom = k_row(before_ref[0], last_ref[0], below_ref[0], kappa_ref[rows - 1])
    for at, value in enumerate((top, bottom)):
        outs[0][at] = value.astype(outs[0].dtype)
        if with_wide:
            outs[1 + at][0] = value


def rows_spec(count, cols, first=0):
    return pl.BlockSpec((count, cols, LANES), lambda j: (first // count, 0, j))


def stencil_mid(x, edges, kappa, with_wide):
    rows, cols = kappa.shape[:2]
    columns = x.shape[2]
    shape = (rows - 2, cols, columns)
    outs = [jax.ShapeDtypeStruct(shape, jnp.bfloat16)]
    if with_wide:
        outs.append(jax.ShapeDtypeStruct(shape, jnp.float32))
    arrays = [x, *edges]
    return pl.pallas_call(
        functools.partial(mid_kernel, rows, with_wide),
        grid=(columns // LANES,),
        in_specs=[rows_spec(a.shape[0], cols) for a in arrays] + [pl.BlockSpec((rows, cols, 1), lambda j: (0, 0, 0))],
        out_specs=[rows_spec(rows - 2, cols) for _ in outs],
        out_shape=outs,
        cost_estimate=pl.CostEstimate(flops=8 * x.size, bytes_accessed=10 * x.size, transcendentals=0),
        name="stencil_mid",
    )(*arrays, kappa)


def stencil_edge(above, first, second, before, last, below, kappa, with_wide):
    rows, cols = kappa.shape[:2]
    columns = above.shape[2]
    outs = [jax.ShapeDtypeStruct((2, cols, columns), jnp.bfloat16)]
    if with_wide:
        outs += [jax.ShapeDtypeStruct((1, cols, columns), jnp.float32)] * 2
    picks = [(above, 0), first, second, before, last, (below, 0)]
    return pl.pallas_call(
        functools.partial(edge_kernel, with_wide),
        grid=(columns // LANES,),
        in_specs=[rows_spec(1, cols, at) for _, at in picks] + [pl.BlockSpec((rows, cols, 1), lambda j: (0, 0, 0))],
        out_specs=[rows_spec(out.shape[0], cols) for out in outs],
        out_shape=outs,
        cost_estimate=pl.CostEstimate(flops=16 * above.size, bytes_accessed=36 * above.size, transcendentals=0),
        name="stencil_edge",
    )(*[array for array, _ in picks], kappa)


def halo(first, last):
    count = lax.axis_size("space")
    forward = [(i, i + 1) for i in range(count - 1)]
    backward = [(target, source) for source, target in forward]
    above = lax.ppermute(last, "space", forward)
    below = lax.ppermute(first, "space", backward)
    return above, below


def gather_pieces(own):
    count = lax.axis_size("species")
    pieces = {0: own}
    for d in range(2, count, 2):
        pieces[d] = xor_swap(own, "species", d)
    for d in range(0, count, 2):
        pieces[d + 1] = xor_swap(pieces[d], "species", 1)
    return [pieces[d] for d in range(count)]


def prior_kernel(pieces, *refs):
    tree_ref, out_ref = refs[2 * pieces], refs[2 * pieces + 1]
    total = None
    for at in range(pieces):
        part = jnp.dot(refs[at][...], refs[pieces + at][...], preferred_element_type=jnp.float32)
        total = part if total is None else total + part
    out_ref[...] = tree_ref[...] - total


def minus_prior(tree, pieces, weights, row_of, block):
    plots, columns = pieces[0].shape
    count = len(pieces)
    held = pl.BlockSpec((block, columns), lambda i: (row_of(i), 0))
    return pl.pallas_call(
        functools.partial(prior_kernel, count),
        grid=(plots // block,),
        in_specs=[pl.BlockSpec((block, columns), lambda i: (i, 0))] * count
        + [pl.BlockSpec((columns, columns), lambda i: (0, 0))] * count
        + [held],
        out_specs=held,
        out_shape=jax.ShapeDtypeStruct(tree.shape, tree.dtype),
        input_output_aliases={2 * count: 0},
        cost_estimate=pl.CostEstimate(
            flops=2 * count * plots * columns * columns, bytes_accessed=16 * plots * columns, transcendentals=0
        ),
        name="prior",
    )(*pieces, *weights, tree)


def sum_over_space(blocks, scale):
    _, block_rows, columns = blocks.shape
    count = lax.axis_size("space")
    outer = count // 2
    per_piece = count // lax.axis_size("species")
    me, mine = lax.axis_index("space"), lax.axis_index("species")
    split = max(16, block_rows * 11 // 16 // 16 * 16)

    def block(target, low, high):
        slot = ((target // per_piece) ^ mine) * per_piece + target % per_piece
        return lax.dynamic_slice(blocks, (slot, low, 0), (1, high - low, columns))

    def pair(low, high, a, b):
        return block(me ^ (2 * a + b), low, high)

    wide = lambda value: value.astype(jnp.float32)
    near_send = jnp.concatenate([pair(0, split, a, 1) for a in range(outer)], axis=0)
    near = xor_swap(near_send, "space", 1)
    far_send = [
        jnp.concatenate([pair(split, block_rows, a, b) for b in range(2)], axis=0) for a in range(1, outer)
    ]
    far = [xor_swap(far_send[a - 1], "space", 2 * a) for a in range(1, outer)]
    near_sum = [wide(pair(0, split, a, 0)[0]) + wide(near[a]) for a in range(outer)]
    near_low = [value.astype(jnp.bfloat16) for value in near_sum]
    near_far = [xor_swap(near_low[a], "space", 2 * a) for a in range(1, outer)]
    far_sum = [wide(pair(split, block_rows, 0, b)[0]) for b in range(2)]
    for part in far:
        far_sum = [far_sum[b] + wide(part[b]) for b in range(2)]
    far_near = xor_swap(far_sum[1].astype(jnp.bfloat16), "space", 1)
    first = near_sum[0]
    for part in near_far:
        first = first + wide(part)
    second = far_sum[0] + wide(far_near)
    return jnp.concatenate([first, second], axis=0) * scale


def shards(effects, kappa_sq, growth, tree_species, tree_counts, noise_precision, species_precision):
    rows, cols, columns = effects.shape
    plots = rows * cols
    slots = growth.shape[2]
    space_count = lax.axis_size("space")
    species_count = lax.axis_size("species")
    mine = lax.axis_index("species")
    kappa = kappa_sq.reshape(rows, cols, 1)
    flat = lambda value: value.reshape(-1, columns)
    above, below = halo(effects[:1], effects[rows - 1 :])
    mid_low, mid_wide = stencil_mid(effects, [], kappa, True)
    mid_pieces = gather_pieces(flat(mid_low))

    tree, tree_parts = None, next(n for n in (3, 2, 1) if rows % n == 0)

    def tree_part(at, before):
        length = plots // tree_parts
        return tree_term(
            effects.reshape(plots, columns),
            growth.reshape(plots, slots),
            tree_species.reshape(plots, slots),
            tree_counts.reshape(plots),
            noise_precision,
            mine * columns,
            at * length,
            length,
            before,
        )

    for at in range(tree_parts):
        tree = tree_part(at, tree)

    edge_low, top_wide, bottom_wide = stencil_edge(
        above, (effects, 0), (effects, 1), (effects, rows - 2), (effects, rows - 1), below, kappa, True
    )
    edge_pieces = gather_pieces(flat(edge_low))
    above_k, below_k = halo(top_wide, bottom_wide)

    (spatial_mid,) = stencil_mid(mid_wide, [top_wide, bottom_wide], kappa, False)
    spatial_mid_pieces = gather_pieces(flat(spatial_mid))

    def product(left, right):
        return lax.dot_general(left, right, (((0,), (0,)), ((), ())), preferred_element_type=jnp.float32)

    grams = []
    for d in range(species_count):
        part = product(mid_pieces[d], mid_pieces[0]) + product(edge_pieces[d], edge_pieces[0])
        grams.append(part.astype(jnp.bfloat16))
    blocks = jnp.stack(grams).reshape(space_count, -1, columns)
    gram = sum_over_space(blocks, -0.5 / (plots * space_count))

    (spatial_edge,) = stencil_edge(
        above_k, (top_wide, 0), (mid_wide, 0), (mid_wide, rows - 3), (bottom_wide, 0), below_k, kappa, False
    )
    spatial_edge_pieces = gather_pieces(flat(spatial_edge))
    weights = [
        lax.dynamic_slice(species_precision, ((mine ^ d) * columns, 0), (columns, columns))
        for d in range(species_count)
    ]
    grad = minus_prior(tree, spatial_mid_pieces, weights, lambda i: i + 1, cols)
    grad = minus_prior(grad, spatial_edge_pieces, weights, lambda i: i * (rows - 1), cols)
    return (grad.reshape(rows, cols, columns), gram)


def solution(mesh):
    return jax.shard_map(
        shards,
        mesh=mesh,
        in_specs=(
            P("space", None, "species"),
            P("space", None),
            P("space", None, None),
            P("space", None, None),
            P("space", None),
            P("species"),
            P(None, "species"),
        ),
        out_specs=(P("space", None, "species"), P("space", "species")),
        check_vma=False,
    )
```

time: 240 us -> 149 us (0.62)
  matrix products: 117 us -> 9.08 us
  Pallas kernels: 0 us -> 54.7 us
  waiting for transfers between devices: 60.3 us -> 34.8 us
  starting transfers between devices: 12.5 us -> 33.3 us
  local copies, waits for them, and re-layouts: 23.5 us -> 7.48 us
  between operations: 13.9 us -> 0.88 us
  other arithmetic: 11.6 us -> 7.09 us
    dot_general x14 -> x8, matrix products: 117 us -> 9.08 us  [product(): lax.dot_general(left, right, (((0,), (0,)), ((), ())), preferred_element_...]
    pallas_call x0 -> x9, Pallas kernels: none -> 54.7 us  [the longest x3 24.8 us: tree_term(): pl.pallas_call(functools.partial(tree_kernel, columns // LANES), grid=(le...]
    ppermute x4 -> x24, starting transfers between devices: 12.2 us -> 33.3 us  [the longest x20 20.5 us: xor_swap(): return lax.ppermute(value, axis, [(i, i ^ mask) for i in range(count)])]
    reduce_scatter x1 -> x0, waiting for transfers between devices: 12.5 us -> none  [shards(): lax.psum_scatter(block_term * gram_scale, 'space', scatter_dimension=0, t...]
    dynamic_update_slice x12 -> x0, local copies, waits for them, and re-layouts: 10.9 us -> none  [shards(): lax.map(block_sums, (local_column.reshape(block_count, block_plots, tree_...]
    another operation x2 -> x0, local copies, waits for them, and re-layouts: 7.74 us -> none  [shards(): jnp.stack([growth_flat, jnp.ones_like(growth_flat)], axis=2)]
    all_gather x2 -> x0, waiting for transfers between devices: 7.52 us -> none  [the longest x1 7.52 us: shards(): effect_piece = lax.all_gather(effects_low, 'species', axis=1, tiled=True)]
    ppermute x4 -> x24, waiting for transfers between devices: 40.3 us -> 34.8 us  [the longest x20 26.6 us: xor_swap(): return lax.ppermute(value, axis, [(i, i ^ mask) for i in range(count)])]
  transfers between devices with their start and end apart: 7 -> 24, of which waited for: 4 -> 8; matrix products, arithmetic and copies ran while one was open for 60% -> 13% of each run, Pallas kernels for 0% -> 37%
where the time goes in v1:
time: 149 us; the launch traced here: 147 us
  Pallas kernels  54.7 us (37%)
  waiting for transfers between devices  34.8 us (23%)
  starting transfers between devices  33.3 us (22%)
  matrix products  9.08 us (6%)
  local copies, waits for them, and re-layouts  7.48 us (5%)
  other arithmetic  7.09 us (5%)
    ppermute x20, waiting for transfers between devices, xor_swap(): return lax.ppermute(value, axis, [(i, i ^ mask) for i in range(count)])  26.6 us
    pallas_call x3, Pallas kernels, tree_term(): pl.pallas_call(functools.partial(tree_kernel, columns // LANES), grid=(le...  24.8 us
    ppermute x20, starting transfers between devices, xor_swap(): return lax.ppermute(value, axis, [(i, i ^ mask) for i in range(count)])  20.5 us
    pallas_call x2, Pallas kernels, minus_prior(): pl.pallas_call(functools.partial(prior_kernel, count), grid=(plots // blo...  11.3 us
    ppermute x2, starting transfers between devices, halo(): above = lax.ppermute(last, 'space', forward)  10.1 us
    pallas_call x2, Pallas kernels, stencil_mid(): pl.pallas_call(functools.partial(mid_kernel, rows, with_wide), grid=(colu...  9.7 us
    dot_general x8, matrix products, product(): lax.dot_general(left, right, (((0,), (0,)), ((), ())), preferred_element_...  9.08 us
    pallas_call x2, Pallas kernels, stencil_edge(): pl.pallas_call(functools.partial(edge_kernel, with_wide), grid=(columns /...  8.94 us
  transfers between devices with their start and end apart: 24, of which 8 were waited for; matrix products, arithmetic and copies ran while one was open for 13% of the time, Pallas kernels for 37%

profile of v1, /device:TPU:0, one launch (start us, length us, event | category | flops | bytes accessed | tf_op | source)
XLA Modules:
  0.0 147.3 jit_solution(6434431567075732385)
XLA Ops:
  0.6 1.3 fusion.15
  1.9 4.9 %collective-permute-start = (f32[1,256,512]{2,1,0:T(8,128)S(1)}, f32[1,256,512]{2,1,0:T(8,128)S(1)}, u32[]{:S(2)}, u32[]{:S(2)}) collective-permute-start(f32[1,256,512]{2,1,0:T(8,128)S(1)} %get-tuple-element.13), channel_id=1, source_target_pairs={{0,4},{4,8},{8,12},{12,16},{16,20},{20,24},{24,28},{1,5},{5,9},{9,... | collective-permute-start | bytes 1572872 | tf_op jit(solution)/shard_map/ppermute | solution.py:171
  6.9 1.3 collective-permute-start.1
  8.2 1.3 copy.15.kappa_ref.refs_1_.refs_3_
  9.4 4.9 %stencil_mid.2 = (bf16[4,256,512]{2,1,0:T(8,128)(2,1)}, f32[4,256,512]{2,1,0:T(8,128)}) custom-call(f32[6,256,512]{2,1,0:T(8,128)} %refs_0_.1, f32[6,256,1]{2,1,0:T(8,128)} %copy.15.kappa_ref.refs_1_.refs_3_), custom_call_target="tpu_custom_call" | custom-call | flops 6291456 | bytes 7864320 | tf_op jit(solution)/shard_map/stencil_mid/pallas_call | solution.py:138
  14.3 1.5 %collective-permute-start.12 = (bf16[1024,512]{1,0:T(8,128)(2,1)}, bf16[1024,512]{1,0:T(8,128)(2,1)}, u32[]{:S(2)}, u32[]{:S(2)}) collective-permute-start(bf16[1024,512]{1,0:T(8,128)(2,1)} %bitcast.99), channel_id=1, source_target_pairs={{0,2},{1,3},{2,0},{3,1},{4,6},{5,7},{6,4},{7,5},{8,10},{9,11},{10,... | collective-permute-start | bytes 3145736 | tf_op jit(solution)/shard_map/ppermute | solution.py:16
  15.8 1.3 copy.27
  17.1 8.2 %tree_term.3.rest_0_ = f32[1536,512]{1,0:T(8,128)} custom-call(s32[1]{0:T(128)} %bitcast.3.first_ref, f32[1536,512]{1,0:T(8,128)} %bitcast.66, f32[1536,128]{1,0:T(8,128)} %bitcast.84, s32[1536,128]{1,0:T(8,128)} %bitcast.87, s32[1536,1]{1,0:T(8,128)} %bitcast.75, f32[1,512]{1,0:T(1,128)} %bitcast.94), custom_call_target="tpu_custom_call" | custom-call | flops 1073741824 | bytes 2621440 | tf_op jit(solution)/shard_map/tree_term/pallas_call | solution.py:72
  25.4 3.8 %collective-permute-done.above_ref = f32[1,256,512]{2,1,0:T(8,128)S(1)} collective-permute-done((f32[1,256,512]{2,1,0:T(8,128)S(1)}, f32[1,256,512]{2,1,0:T(8,128)S(1)}, u32[]{:S(2)}, u32[]{:S(2)}) %collective-permute-start) | collective-permute-done | bytes 524320 | tf_op jit(solution)/shard_map/ppermute | solution.py:171
  29.2 0.8 copy-done.4
  30.0 0.8 copy-done.5
  30.8 4.5 %stencil_edge.2 = (bf16[2,256,512]{2,1,0:T(8,128)(2,1)}, f32[1,256,512]{2,1,0:T(8,128)}, f32[1,256,512]{2,1,0:T(8,128)}) custom-call(f32[1,256,512]{2,1,0:T(8,128)} %copy-done.4, f32[6,256,512]{2,1,0:T(8,128)} %refs_0_.1, f32[6,256,512]{2,1,0:T(8,128)} %refs_0_.1, f32[6,256,512]{2,1,0:T(8,128)} %refs_0_.1, f32[6,256,512]{2,1,0:T(8,128)} %refs_0_.1, ...), custom_call_target="tpu_custom_call" | custom-call | flops 2097152 | bytes 4718592 | tf_op jit(solution)/shard_map/stencil_edge/pallas_call | solution.py:156
  35.4 1.6 %collective-permute-start.13 = (bf16[512,512]{1,0:T(8,128)(2,1)}, bf16[512,512]{1,0:T(8,128)(2,1)S(1)}, u32[]{:S(2)}, u32[]{:S(2)}) collective-permute-start(bf16[512,512]{1,0:T(8,128)(2,1)} %bitcast.70), channel_id=1, source_target_pairs={{0,2},{1,3},{2,0},{3,1},{4,6},{5,7},{6,4},{7,5},{8,10},{9,11},{10,... | collective-permute-start | bytes 1572872 | tf_op jit(solution)/shard_map/ppermute | solution.py:16
  36.9 5.2 %collective-permute-start.2 = (f32[1,256,512]{2,1,0:T(8,128)}, f32[1,256,512]{2,1,0:T(8,128)}, u32[]{:S(2)}, u32[]{:S(2)}) collective-permute-start(f32[1,256,512]{2,1,0:T(8,128)} %get-tuple-element.7.last_ref.refs_2_), channel_id=1, source_target_pairs={{0,4},{4,8},{8,12},{12,16},{16,20},{20,24},{24,28},{1,5},{5,9},{9,... | collective-permute-start | bytes 1572872 | tf_op jit(solution)/shard_map/ppermute | solution.py:171
  42.1 1.4 collective-permute-start.3
  43.5 8.3 %tree_term.4.rest_0_ = f32[1536,512]{1,0:T(8,128)} custom-call(s32[1]{0:T(128)} %bitcast.3.first_ref, f32[1536,512]{1,0:T(8,128)} %bitcast.67, f32[1536,128]{1,0:T(8,128)} %bitcast.85, s32[1536,128]{1,0:T(8,128)} %bitcast.88, s32[1536,1]{1,0:T(8,128)} %bitcast.76, f32[1,512]{1,0:T(1,128)} %bitcast.95, ...), custom_call_target="tpu_custom_call", output_to_operand_aliasing={{}: (6, {})} | custom-call | flops 1073741824 | bytes 2621440 | tf_op jit(solution)/shard_map/tree_term/pallas_call | solution.py:72
  51.8 0.7 convolution_bitcast_fusion.1
  52.5 4.8 %stencil_mid.3 = bf16[4,256,512]{2,1,0:T(8,128)(2,1)} custom-call(f32[4,256,512]{2,1,0:T(8,128)} %get-tuple-element.9.second_ref.before_ref.refs_0_, f32[1,256,512]{2,1,0:T(8,128)} %get-tuple-element.8.first_ref.refs_1_, f32[1,256,512]{2,1,0:T(8,128)} %get-tuple-element.7.last_ref.refs_2_, f32[6,256,1]{2,1,0:T(8,128)} %copy.15.kappa_ref.refs_1_.refs_3_), custom_call_target="tpu_custom_call" | custom-call | flops 4194304 | bytes 5242880 | tf_op jit(solution)/shard_map/stencil_mid/pallas_call | solution.py:138
  57.4 1.3 fusion.5
  58.6 4.4 %collective-permute-done.2.above_ref = f32[1,256,512]{2,1,0:T(8,128)} collective-permute-done((f32[1,256,512]{2,1,0:T(8,128)}, f32[1,256,512]{2,1,0:T(8,128)}, u32[]{:S(2)}, u32[]{:S(2)}) %collective-permute-start.2) | collective-permute-done | bytes 524320 | tf_op jit(solution)/shard_map/ppermute | solution.py:171
  63.6 4.4 %stencil_edge.3 = bf16[2,256,512]{2,1,0:T(8,128)(2,1)} custom-call(f32[1,256,512]{2,1,0:T(8,128)} %collective-permute-done.2.above_ref, f32[1,256,512]{2,1,0:T(8,128)} %get-tuple-element.8.first_ref.refs_1_, f32[4,256,512]{2,1,0:T(8,128)} %get-tuple-element.9.second_ref.before_ref.refs_0_, f32[4,256,512]{2,1,0:T(8,128)} %get-tuple-element.9.second_ref.before_ref.refs_0_, ...), custom_call_target="tpu_custom_call" | custom-call | flops 2097152 | bytes 4718592 | tf_op jit(solution)/shard_map/stencil_edge/pallas_call | solution.py:156
  69.2 2.0 %fusion.7 = bf16[1,512,512]{2,1,0:T(8,128)(2,1)S(1)} fusion(f32[512,512]{1,0:T(8,128)S(1)} %fusion.17, bf16[1024,512]{1,0:T(8,128)(2,1)} %collective-permute-done.12, bf16[1024,512]{1,0:T(8,128)(2,1)S(1)} %bitcast.101), kind=kOutput, calls=%fused_computation.13 | convolution fusion | flops 537395200 | bytes 3670016 | tf_op jit(solution)/shard_map/dot_general | solution.py:293
  71.4 1.5 %fusion.16 = f32[512,512]{1,0:T(8,128)S(1)} fusion(bf16[512,512]{1,0:T(8,128)(2,1)} %collective-permute-done.11, bf16[512,512]{1,0:T(8,128)(2,1)S(1)} %bitcast.73), kind=kOutput, calls=%fused_computation.47 | convolution fusion | flops 268435456 | bytes 2097152 | tf_op jit(solution)/shard_map/dot_general | solution.py:293
  72.9 1.5 %collective-permute-start.5 = (bf16[512,512]{1,0:T(8,128)(2,1)}, bf16[512,512]{1,0:T(8,128)(2,1)}, u32[]{:S(2)}, u32[]{:S(2)}) collective-permute-start(bf16[512,512]{1,0:T(8,128)(2,1)} %bitcast.1.refs_0_), channel_id=1, source_target_pairs={{0,2},{1,3},{2,0},{3,1},{4,6},{5,7},{6,4},{7,5},{8,10},{9,11},{10,... | collective-permute-start | bytes 1572872 | tf_op jit(solution)/shard_map/ppermute | solution.py:16
  74.5 2.0 %fusion.8 = bf16[1,512,512]{2,1,0:T(8,128)(2,1)S(1)} fusion(f32[512,512]{1,0:T(8,128)S(1)} %fusion.16, bf16[1024,512]{1,0:T(8,128)(2,1)} %collective-permute-done.10, bf16[1024,512]{1,0:T(8,128)(2,1)S(1)} %bitcast.102), kind=kOutput, calls=%fused_computation.14 | convolution fusion | flops 537395200 | bytes 3670016 | tf_op jit(solution)/shard_map/dot_general | solution.py:293
  76.4 12.8 %collective-permute-done.8.refs_2_ = bf16[1024,512]{1,0:T(8,128)(2,1)} collective-permute-done((bf16[1024,512]{1,0:T(8,128)(2,1)S(1)}, bf16[1024,512]{1,0:T(8,128)(2,1)}, u32[]{:S(2)}, u32[]{:S(2)}) %collective-permute-start.8) | collective-permute-done | bytes 1048608 | tf_op jit(solution)/shard_map/ppermute | solution.py:16
  89.7 0.7 fusion.6
  91.2 4.6 %collective-permute-start.20 = (bf16[2,80,512]{2,1,0:T(8,128)(2,1)S(1)}, bf16[2,80,512]{2,1,0:T(8,128)(2,1)S(1)}, u32[]{:S(2)}, u32[]{:S(2)}) collective-permute-start(bf16[2,80,512]{2,1,0:T(8,128)(2,1)S(1)} %pad_maximum_fusion.2), channel_id=1, source_target_pairs={{0,8},{4,12},{8,0},{12,4},{16,24},{20,28},{24,16},{28,20},{1,9},{5... | collective-permute-start | bytes 491528 | tf_op jit(solution)/shard_map/ppermute | solution.py:16
  95.7 2.7 %collective-permute-start.21 = (bf16[2,80,512]{2,1,0:T(8,128)(2,1)S(1)}, bf16[2,80,512]{2,1,0:T(8,128)(2,1)S(1)}, u32[]{:S(2)}, u32[]{:S(2)}) collective-permute-start(bf16[2,80,512]{2,1,0:T(8,128)(2,1)S(1)} %pad_maximum_fusion.3), channel_id=1, source_target_pairs={{0,16},{4,20},{8,24},{12,28},{16,0},{20,4},{24,8},{28,12},{1,17},{... | collective-permute-start | bytes 491528 | tf_op jit(solution)/shard_map/ppermute | solution.py:16
  98.4 1.0 pad_maximum_fusion.1
  99.4 4.5 %collective-permute-done.20 = bf16[2,80,512]{2,1,0:T(8,128)(2,1)S(1)} collective-permute-done((bf16[2,80,512]{2,1,0:T(8,128)(2,1)S(1)}, bf16[2,80,512]{2,1,0:T(8,128)(2,1)S(1)}, u32[]{:S(2)}, u32[]{:S(2)}) %collective-permute-start.20) | collective-permute-done | bytes 163872 | tf_op jit(solution)/shard_map/ppermute | solution.py:16
  103.9 2.7 %collective-permute-done.21 = bf16[2,80,512]{2,1,0:T(8,128)(2,1)S(1)} collective-permute-done((bf16[2,80,512]{2,1,0:T(8,128)(2,1)S(1)}, bf16[2,80,512]{2,1,0:T(8,128)(2,1)S(1)}, u32[]{:S(2)}, u32[]{:S(2)}) %collective-permute-start.21) | collective-permute-done | bytes 163872 | tf_op jit(solution)/shard_map/ppermute | solution.py:16
  106.6 2.5 %collective-permute-start.22 = (bf16[2,80,512]{2,1,0:T(8,128)(2,1)S(1)}, bf16[2,80,512]{2,1,0:T(8,128)(2,1)}, u32[]{:S(2)}, u32[]{:S(2)}) collective-permute-start(bf16[2,80,512]{2,1,0:T(8,128)(2,1)S(1)} %pad_maximum_fusion.4), channel_id=1, source_target_pairs={{0,24},{4,28},{8,16},{12,20},{16,8},{20,12},{24,0},{28,4},{1,25},{... | collective-permute-start | bytes 491528 | tf_op jit(solution)/shard_map/ppermute | solution.py:16
  109.1 1.4 constant_dynamic-slice_fusion.10
  110.5 3.4 %collective-permute-done.22 = bf16[2,80,512]{2,1,0:T(8,128)(2,1)} collective-permute-done((bf16[2,80,512]{2,1,0:T(8,128)(2,1)S(1)}, bf16[2,80,512]{2,1,0:T(8,128)(2,1)}, u32[]{:S(2)}, u32[]{:S(2)}) %collective-permute-start.22) | collective-permute-done | bytes 163872 | tf_op jit(solution)/shard_map/ppermute | solution.py:16
  113.9 0.9 fusion.14
  114.9 8.3 %tree_term.5.refs_8_ = f32[1536,512]{1,0:T(8,128)} custom-call(s32[1]{0:T(128)} %bitcast.3.first_ref, f32[1536,512]{1,0:T(8,128)} %bitcast.68, f32[1536,128]{1,0:T(8,128)} %bitcast.86, s32[1536,128]{1,0:T(8,128)} %bitcast.89, s32[1536,1]{1,0:T(8,128)} %bitcast.77, f32[1,512]{1,0:T(1,128)} %bitcast.96, ...), custom_call_target="tpu_custom_call", output_to_operand_aliasing={{}: (6, {})} | custom-call | flops 1073741824 | bytes 2621440 | tf_op jit(solution)/shard_map/tree_term/pallas_call | solution.py:72
  123.3 0.7 collective-permute-done.23
  124.0 1.0 bitcast_add_fusion.1
  125.0 2.0 %fusion.11 = (bf16[176,512]{1,0:T(8,128)(2,1)}, bf16[176,512]{1,0:T(8,128)(2,1)}, bf16[176,512]{1,0:T(8,128)(2,1)}) fusion(bf16[4,176,512]{2,1,0:T(8,128)(2,1)} %collective-permute-done.16, bf16[8,256,512]{2,1,0:T(8,128)(2,1)S(1)} %bitcast.82, s32[]{:T(128)S(6)} %select_n.149, s32[]{:T(128)S(6)} %select_n.155, s32[]{:T(128)S(6)} %select_n.152), kind=kLoop, calls=%fused_computation.23 | loop fusion | flops 1081344 | bytes 1622028 | tf_op jit(solution)/shard_map/convert_element_type | solution.py:238
  127.0 2.2 %collective-permute-start.17 = (bf16[176,512]{1,0:T(8,128)(2,1)}, bf16[176,512]{1,0:T(8,128)(2,1)S(1)}, u32[]{:S(2)}, u32[]{:S(2)}) collective-permute-start(bf16[176,512]{1,0:T(8,128)(2,1)} %get-tuple-element.14), channel_id=1, source_target_pairs={{0,8},{4,12},{8,0},{12,4},{16,24},{20,28},{24,16},{28,20},{1,9},{5... | collective-permute-start | bytes 540680 | tf_op jit(solution)/shard_map/ppermute | solution.py:16
  129.2 0.8 collective-permute-start.18
  130.0 1.6 %collective-permute-start.19 = (bf16[176,512]{1,0:T(8,128)(2,1)}, bf16[176,512]{1,0:T(8,128)(2,1)S(1)}, u32[]{:S(2)}, u32[]{:S(2)}) collective-permute-start(bf16[176,512]{1,0:T(8,128)(2,1)} %get-tuple-element.15), channel_id=1, source_target_pairs={{0,24},{4,28},{8,16},{12,20},{16,8},{20,12},{24,0},{28,4},{1,25},{... | collective-permute-start | bytes 540680 | tf_op jit(solution)/shard_map/ppermute | solution.py:16
  131.6 6.8 %prior.2.refs_8_ = f32[1536,512]{1,0:T(8,128)} custom-call(bf16[1024,512]{1,0:T(8,128)(2,1)} %bitcast.90, bf16[1024,512]{1,0:T(8,128)(2,1)} %collective-permute-done.7.refs_1_, bf16[1024,512]{1,0:T(8,128)(2,1)} %collective-permute-done.8.refs_2_, bf16[1024,512]{1,0:T(8,128)(2,1)} %collective-permute-done.9.refs_3_, ...), custom_call_target="tpu_custom_call", output_to_operand_aliasing={{}: (8, {})} | custom-call | flops 2147483648 | bytes 8388608 | tf_op jit(solution)/shard_map/prior/pallas_call | solution.py:199
  138.4 4.5 %prior.3 = f32[1536,512]{1,0:T(8,128)} custom-call(bf16[512,512]{1,0:T(8,128)(2,1)} %bitcast.1.refs_0_, bf16[512,512]{1,0:T(8,128)(2,1)} %collective-permute-done.4.refs_1_, bf16[512,512]{1,0:T(8,128)(2,1)} %collective-permute-done.5.refs_2_, bf16[512,512]{1,0:T(8,128)(2,1)} %collective-permute-done.6.refs_3_, ...), custom_call_target="tpu_custom_call", output_to_operand_aliasing={{}: (8, {})} | custom-call | flops 1073741824 | bytes 4194304 | tf_op jit(solution)/shard_map/prior/pallas_call | solution.py:199
  142.9 2.5 %collective-permute-done.18 = bf16[176,512]{1,0:T(8,128)(2,1)S(1)} collective-permute-done((bf16[176,512]{1,0:T(8,128)(2,1)}, bf16[176,512]{1,0:T(8,128)(2,1)S(1)}, u32[]{:S(2)}, u32[]{:S(2)}) %collective-permute-start.18) | collective-permute-done | bytes 180256 | tf_op jit(solution)/shard_map/ppermute | solution.py:16
  145.4 1.0 fusion.10
  146.5 0.8 maximum_multiply_fusion
  (56 shorter events, 3.5 us)
Async XLA Ops:
  0.6 7.5 %copy-start.7 = (f32[6,256]{1,0:T(8,128)S(1)}, f32[6,256]{1,0:T(8,128)}, u32[]{:S(2)}) copy-start(f32[6,256]{1,0:T(8,128)} %param.8) | copy-start | bytes 18436
  1.9 27.3 %collective-permute-start = (f32[1,256,512]{2,1,0:T(8,128)S(1)}, f32[1,256,512]{2,1,0:T(8,128)S(1)}, u32[]{:S(2)}, u32[]{:S(2)}) collective-permute-start(f32[1,256,512]{2,1,0:T(8,128)S(1)} %get-tuple-element.13), channel_id=1, source_target_pairs={{0,4},{4,8},{8,12},{12,16},{16,20},{20,24},{24,28},{1,5},{5,9},{9,... | collective-permute-start | bytes 1572872 | tf_op jit(solution)/shard_map/ppermute | solution.py:171
  6.9 22.4 %collective-permute-start.1 = (f32[1,256,512]{2,1,0:T(8,128)S(1)}, f32[1,256,512]{2,1,0:T(8,128)S(1)}, u32[]{:S(2)}, u32[]{:S(2)}) collective-permute-start(f32[1,256,512]{2,1,0:T(8,128)S(1)} %get-tuple-element.12), channel_id=1, source_target_pairs={{4,0},{8,4},{12,8},{16,12},{20,16},{24,20},{28,24},{5,1},{9,5},{13... | collective-permute-start | bytes 1572872 | tf_op jit(solution)/shard_map/ppermute | solution.py:172
  9.4 6.4 %copy-start.8 = (s32[6,256]{1,0:T(8,128)S(1)}, s32[6,256]{1,0:T(8,128)}, u32[]{:S(2)}) copy-start(s32[6,256]{1,0:T(8,128)} %param.11) | copy-start | bytes 18436
  14.3 53.9 %collective-permute-start.12 = (bf16[1024,512]{1,0:T(8,128)(2,1)}, bf16[1024,512]{1,0:T(8,128)(2,1)}, u32[]{:S(2)}, u32[]{:S(2)}) collective-permute-start(bf16[1024,512]{1,0:T(8,128)(2,1)} %bitcast.99), channel_id=1, source_target_pairs={{0,2},{1,3},{2,0},{3,1},{4,6},{5,7},{6,4},{7,5},{8,10},{9,11},{10,... | collective-permute-start | bytes 3145736 | tf_op jit(solution)/shard_map/ppermute | solution.py:16
  15.8 57.1 %collective-permute-start.10 = (bf16[1024,512]{1,0:T(8,128)(2,1)}, bf16[1024,512]{1,0:T(8,128)(2,1)}, u32[]{:S(2)}, u32[]{:S(2)}) collective-permute-start(bf16[1024,512]{1,0:T(8,128)(2,1)} %bitcast.100), channel_id=1, source_target_pairs={{0,1},{1,0},{2,3},{3,2},{4,5},{5,4},{6,7},{7,6},{8,9},{9,8},{10,11... | collective-permute-start | bytes 3145736 | tf_op jit(solution)/shard_map/ppermute | solution.py:16
  29.2 0.8 copy-start.4
  30.0 0.8 copy-start.5
  35.4 32.6 %collective-permute-start.13 = (bf16[512,512]{1,0:T(8,128)(2,1)}, bf16[512,512]{1,0:T(8,128)(2,1)S(1)}, u32[]{:S(2)}, u32[]{:S(2)}) collective-permute-start(bf16[512,512]{1,0:T(8,128)(2,1)} %bitcast.70), channel_id=1, source_target_pairs={{0,2},{1,3},{2,0},{3,1},{4,6},{5,7},{6,4},{7,5},{8,10},{9,11},{10,... | collective-permute-start | bytes 1572872 | tf_op jit(solution)/shard_map/ppermute | solution.py:16
  36.9 26.1 %collective-permute-start.2 = (f32[1,256,512]{2,1,0:T(8,128)}, f32[1,256,512]{2,1,0:T(8,128)}, u32[]{:S(2)}, u32[]{:S(2)}) collective-permute-start(f32[1,256,512]{2,1,0:T(8,128)} %get-tuple-element.7.last_ref.refs_2_), channel_id=1, source_target_pairs={{0,4},{4,8},{8,12},{12,16},{16,20},{20,24},{24,28},{1,5},{5,9},{9,... | collective-permute-start | bytes 1572872 | tf_op jit(solution)/shard_map/ppermute | solution.py:171
  42.1 9.7 %copy-start.9 = (bf16[4,256,512]{2,1,0:T(8,128)(2,1)S(1)}, bf16[4,256,512]{2,1,0:T(8,128)(2,1)}, u32[]{:S(2)}) copy-start(bf16[4,256,512]{2,1,0:T(8,128)(2,1)} %get-tuple-element.10) | copy-start | bytes 3145732
  42.1 20.9 %collective-permute-start.3 = (f32[1,256,512]{2,1,0:T(8,128)}, f32[1,256,512]{2,1,0:T(8,128)}, u32[]{:S(2)}, u32[]{:S(2)}) collective-permute-start(f32[1,256,512]{2,1,0:T(8,128)} %get-tuple-element.8.first_ref.refs_1_), channel_id=1, source_target_pairs={{4,0},{8,4},{12,8},{16,12},{20,16},{24,20},{28,24},{5,1},{9,5},{13... | collective-permute-start | bytes 1572872 | tf_op jit(solution)/shard_map/ppermute | solution.py:172
  52.5 4.8 %copy-start = (bf16[2,256,512]{2,1,0:T(8,128)(2,1)S(1)}, bf16[2,256,512]{2,1,0:T(8,128)(2,1)}, u32[]{:S(2)}) copy-start(bf16[2,256,512]{2,1,0:T(8,128)(2,1)} %get-tuple-element.11) | copy-start | bytes 1572868
  57.4 5.6 %copy-start.1 = (bf16[4,256,512]{2,1,0:T(8,128)(2,1)S(1)}, bf16[4,256,512]{2,1,0:T(8,128)(2,1)}, u32[]{:S(2)}) copy-start(bf16[4,256,512]{2,1,0:T(8,128)(2,1)} %stencil_mid.3) | copy-start | bytes 3145732
  63.0 8.2 %collective-permute-start.11 = (bf16[512,512]{1,0:T(8,128)(2,1)S(1)}, bf16[512,512]{1,0:T(8,128)(2,1)}, u32[]{:S(2)}, u32[]{:S(2)}) collective-permute-start(bf16[512,512]{1,0:T(8,128)(2,1)S(1)} %bitcast.71), channel_id=1, source_target_pairs={{0,1},{1,0},{2,3},{3,2},{4,5},{5,4},{6,7},{7,6},{8,9},{9,8},{10,11... | collective-permute-start | bytes 1572872 | tf_op jit(solution)/shard_map/ppermute | solution.py:16
  63.0 26.2 %collective-permute-start.8 = (bf16[1024,512]{1,0:T(8,128)(2,1)S(1)}, bf16[1024,512]{1,0:T(8,128)(2,1)}, u32[]{:S(2)}, u32[]{:S(2)}) collective-permute-start(bf16[1024,512]{1,0:T(8,128)(2,1)S(1)} %bitcast.91), channel_id=1, source_target_pairs={{0,2},{1,3},{2,0},{3,1},{4,6},{5,7},{6,4},{7,5},{8,10},{9,11},{10,... | collective-permute-start | bytes 3145736 | tf_op jit(solution)/shard_map/ppermute | solution.py:16
  68.0 1.2 copy-start.10
  68.0 61.2 %collective-permute-start.7 = (bf16[1024,512]{1,0:T(8,128)(2,1)S(1)}, bf16[1024,512]{1,0:T(8,128)(2,1)}, u32[]{:S(2)}, u32[]{:S(2)}) collective-permute-start(bf16[1024,512]{1,0:T(8,128)(2,1)S(1)} %bitcast.92), channel_id=1, source_target_pairs={{0,1},{1,0},{2,3},{3,2},{4,5},{5,4},{6,7},{7,6},{8,9},{9,8},{10,11... | collective-permute-start | bytes 3145736 | tf_op jit(solution)/shard_map/ppermute | solution.py:16
  68.2 21.4 %collective-permute-start.14 = (bf16[1024,512]{1,0:T(8,128)(2,1)}, bf16[1024,512]{1,0:T(8,128)(2,1)S(1)}, u32[]{:S(2)}, u32[]{:S(2)}) collective-permute-start(bf16[1024,512]{1,0:T(8,128)(2,1)} %collective-permute-done.12), channel_id=1, source_target_pairs={{0,1},{1,0},{2,3},{3,2},{4,5},{5,4},{6,7},{7,6},{8,9},{9,8},{10,11... | collective-permute-start | bytes 3145736 | tf_op jit(solution)/shard_map/ppermute | solution.py:16
  71.2 18.0 %collective-permute-start.15 = (bf16[512,512]{1,0:T(8,128)(2,1)S(1)}, bf16[512,512]{1,0:T(8,128)(2,1)S(1)}, u32[]{:S(2)}, u32[]{:S(2)}) collective-permute-start(bf16[512,512]{1,0:T(8,128)(2,1)S(1)} %collective-permute-done.13), channel_id=1, source_target_pairs={{0,1},{1,0},{2,3},{3,2},{4,5},{5,4},{6,7},{7,6},{8,9},{9,8},{10,11... | collective-permute-start | bytes 1572872 | tf_op jit(solution)/shard_map/ppermute | solution.py:16
  72.9 50.3 %collective-permute-start.5 = (bf16[512,512]{1,0:T(8,128)(2,1)}, bf16[512,512]{1,0:T(8,128)(2,1)}, u32[]{:S(2)}, u32[]{:S(2)}) collective-permute-start(bf16[512,512]{1,0:T(8,128)(2,1)} %bitcast.1.refs_0_), channel_id=1, source_target_pairs={{0,2},{1,3},{2,0},{3,1},{4,6},{5,7},{6,4},{7,5},{8,10},{9,11},{10,... | collective-permute-start | bytes 1572872 | tf_op jit(solution)/shard_map/ppermute | solution.py:16
  89.2 40.8 %collective-permute-start.9 = (bf16[1024,512]{1,0:T(8,128)(2,1)}, bf16[1024,512]{1,0:T(8,128)(2,1)}, u32[]{:S(2)}, u32[]{:S(2)}) collective-permute-start(bf16[1024,512]{1,0:T(8,128)(2,1)} %collective-permute-done.8.refs_2_), channel_id=1, source_target_pairs={{0,1},{1,0},{2,3},{3,2},{4,5},{5,4},{6,7},{7,6},{8,9},{9,8},{10,11... | collective-permute-start | bytes 3145736 | tf_op jit(solution)/shard_map/ppermute | solution.py:16
  89.7 1.0 copy-start.3
  91.0 18.1 %copy-start.2 = (bf16[2048,512]{1,0:T(8,128)(2,1)S(1)}, bf16[2048,512]{1,0:T(8,128)(2,1)}, u32[]{:S(2)}) copy-start(bf16[2048,512]{1,0:T(8,128)(2,1)} %param.13) | copy-start | bytes 6291460
  91.2 12.8 %collective-permute-start.20 = (bf16[2,80,512]{2,1,0:T(8,128)(2,1)S(1)}, bf16[2,80,512]{2,1,0:T(8,128)(2,1)S(1)}, u32[]{:S(2)}, u32[]{:S(2)}) collective-permute-start(bf16[2,80,512]{2,1,0:T(8,128)(2,1)S(1)} %pad_maximum_fusion.2), channel_id=1, source_target_pairs={{0,8},{4,12},{8,0},{12,4},{16,24},{20,28},{24,16},{28,20},{1,9},{5... | collective-permute-start | bytes 491528 | tf_op jit(solution)/shard_map/ppermute | solution.py:16
  95.7 10.8 %collective-permute-start.21 = (bf16[2,80,512]{2,1,0:T(8,128)(2,1)S(1)}, bf16[2,80,512]{2,1,0:T(8,128)(2,1)S(1)}, u32[]{:S(2)}, u32[]{:S(2)}) collective-permute-start(bf16[2,80,512]{2,1,0:T(8,128)(2,1)S(1)} %pad_maximum_fusion.3), channel_id=1, source_target_pairs={{0,16},{4,20},{8,24},{12,28},{16,0},{20,4},{24,8},{28,12},{1,17},{... | collective-permute-start | bytes 491528 | tf_op jit(solution)/shard_map/ppermute | solution.py:16
  103.9 21.1 %collective-permute-start.16 = (bf16[4,176,512]{2,1,0:T(8,128)(2,1)}, bf16[4,176,512]{2,1,0:T(8,128)(2,1)}, u32[]{:S(2)}, u32[]{:S(2)}) collective-permute-start(bf16[4,176,512]{2,1,0:T(8,128)(2,1)} %pad_maximum_fusion.1), channel_id=1, source_target_pairs={{0,4},{4,0},{8,12},{12,8},{16,20},{20,16},{24,28},{28,24},{1,5},{5... | collective-permute-start | bytes 2162696 | tf_op jit(solution)/shard_map/ppermute | solution.py:16
  106.6 16.6 %copy-start.6 = (bf16[2,80,512]{2,1,0:T(8,128)(2,1)}, bf16[2,80,512]{2,1,0:T(8,128)(2,1)S(1)}, u32[]{:S(2)}) copy-start(bf16[2,80,512]{2,1,0:T(8,128)(2,1)S(1)} %collective-permute-done.21) | copy-start | bytes 491524
  106.6 7.3 %collective-permute-start.22 = (bf16[2,80,512]{2,1,0:T(8,128)(2,1)S(1)}, bf16[2,80,512]{2,1,0:T(8,128)(2,1)}, u32[]{:S(2)}, u32[]{:S(2)}) collective-permute-start(bf16[2,80,512]{2,1,0:T(8,128)(2,1)S(1)} %pad_maximum_fusion.4), channel_id=1, source_target_pairs={{0,24},{4,28},{8,16},{12,20},{16,8},{20,12},{24,0},{28,4},{1,25},{... | collective-permute-start | bytes 491528 | tf_op jit(solution)/shard_map/ppermute | solution.py:16
  114.9 9.1 %collective-permute-start.23 = (bf16[80,512]{1,0:T(8,128)(2,1)S(1)}, bf16[80,512]{1,0:T(8,128)(2,1)}, u32[]{:S(2)}, u32[]{:S(2)}) collective-permute-start(bf16[80,512]{1,0:T(8,128)(2,1)S(1)} %fusion.14), channel_id=1, source_target_pairs={{0,4},{4,0},{8,12},{12,8},{16,20},{20,16},{24,28},{28,24},{1,5},{5... | collective-permute-start | bytes 245768 | tf_op jit(solution)/shard_map/ppermute | solution.py:16
  123.2 15.2 %collective-permute-start.4 = (bf16[512,512]{1,0:T(8,128)(2,1)}, bf16[512,512]{1,0:T(8,128)(2,1)}, u32[]{:S(2)}, u32[]{:S(2)}) collective-permute-start(bf16[512,512]{1,0:T(8,128)(2,1)} %bitcast.1.refs_0_), channel_id=1, source_target_pairs={{0,1},{1,0},{2,3},{3,2},{4,5},{5,4},{6,7},{7,6},{8,9},{9,8},{10,11... | collective-permute-start | bytes 1572872 | tf_op jit(solution)/shard_map/ppermute | solution.py:16
  124.0 14.5 %collective-permute-start.6 = (bf16[512,512]{1,0:T(8,128)(2,1)}, bf16[512,512]{1,0:T(8,128)(2,1)}, u32[]{:S(2)}, u32[]{:S(2)}) collective-permute-start(bf16[512,512]{1,0:T(8,128)(2,1)} %collective-permute-done.5.refs_2_), channel_id=1, source_target_pairs={{0,1},{1,0},{2,3},{3,2},{4,5},{5,4},{6,7},{7,6},{8,9},{9,8},{10,11... | collective-permute-start | bytes 1572872 | tf_op jit(solution)/shard_map/ppermute | solution.py:16
  127.0 15.9 %collective-permute-start.17 = (bf16[176,512]{1,0:T(8,128)(2,1)}, bf16[176,512]{1,0:T(8,128)(2,1)S(1)}, u32[]{:S(2)}, u32[]{:S(2)}) collective-permute-start(bf16[176,512]{1,0:T(8,128)(2,1)} %get-tuple-element.14), channel_id=1, source_target_pairs={{0,8},{4,12},{8,0},{12,4},{16,24},{20,28},{24,16},{28,20},{1,9},{5... | collective-permute-start | bytes 540680 | tf_op jit(solution)/shard_map/ppermute | solution.py:16
  129.2 16.3 %collective-permute-start.18 = (bf16[176,512]{1,0:T(8,128)(2,1)}, bf16[176,512]{1,0:T(8,128)(2,1)S(1)}, u32[]{:S(2)}, u32[]{:S(2)}) collective-permute-start(bf16[176,512]{1,0:T(8,128)(2,1)} %get-tuple-element.16), channel_id=1, source_target_pairs={{0,16},{4,20},{8,24},{12,28},{16,0},{20,4},{24,8},{28,12},{1,17},{... | collective-permute-start | bytes 540680 | tf_op jit(solution)/shard_map/ppermute | solution.py:16
  130.0 15.4 %collective-permute-start.19 = (bf16[176,512]{1,0:T(8,128)(2,1)}, bf16[176,512]{1,0:T(8,128)(2,1)S(1)}, u32[]{:S(2)}, u32[]{:S(2)}) collective-permute-start(bf16[176,512]{1,0:T(8,128)(2,1)} %get-tuple-element.15), channel_id=1, source_target_pairs={{0,24},{4,28},{8,16},{12,20},{16,8},{20,12},{24,0},{28,4},{1,25},{... | collective-permute-start | bytes 540680 | tf_op jit(solution)/shard_map/ppermute | solution.py:16

commit v2 on v1

--- a/solution.py
+++ b/solution.py
@@ -16,7 +16,7 @@
     return lax.ppermute(value, axis, [(i, i ^ mask) for i in range(count)])
 
 
-def tree_kernel(groups, first_ref, effects_ref, growth_ref, species_ref, counts_ref, noise_ref, *rest):
+def tree_kernel(groups, first_block, first_ref, effects_ref, growth_ref, species_ref, counts_ref, noise_ref, *rest):
     out_ref = rest[-1]
     rows, slots = growth_ref.shape
     bits = LANES.bit_length() - 1
@@ -26,13 +26,18 @@
     slot_iota = lax.broadcasted_iota(jnp.int32, (8, slots), 1)
     row_iota = lax.broadcasted_iota(jnp.int32, (8, slots), 0)
     one, zero = jnp.bfloat16(1.0), jnp.bfloat16(0.0)
-    first_column = first_ref[0]
+    first_column = first_ref[3]
+    base, per_row = (first_block + pl.program_id(0)) * rows, counts_ref.shape[1]
 
     def step(index, carry):
         at = pl.ds(pl.multiple_of(index * 8, 8), 8)
         local = species_ref[at, :] - first_column
         group = local >> bits
-        valid = (slot_iota < counts_ref[at, :]) & (group >= 0) & (group < groups)
+        grid_row, grid_col = (base + index * 8) // per_row, (base + index * 8) % per_row
+        counts = jnp.full((8, slots), counts_ref[grid_row, grid_col])
+        for plot in range(1, 8):
+            counts = jnp.where(row_iota == plot, counts_ref[grid_row, grid_col + plot], counts)
+        valid = (slot_iota < counts) & (group >= 0) & (group < groups)
         code = jnp.where(valid, group * 8 + row_iota, -1).astype(jnp.float32)
         low = (local & (LANES - 1)).astype(jnp.float32)
         value = growth_ref[at, :].astype(jnp.bfloat16).astype(jnp.float32)
@@ -47,11 +52,11 @@
                 jnp.concatenate([jnp.where(match, value_row, zero), jnp.where(match, one, zero)], axis=0)
             )
         sums = lax.dot_general(
+            jnp.concatenate(rights, axis=1),
             jnp.concatenate(lefts, axis=1),
-            jnp.concatenate(rights, axis=1),
             (((1,), (1,)), ((), ())),
             preferred_element_type=jnp.float32,
-        )
+        ).T
         for group_at in range(groups):
             cols = pl.ds(group_at * LANES, LANES)
             growth_sum = sums[group_at * 8 : group_at * 8 + 8]
@@ -62,7 +67,7 @@
     lax.fori_loop(0, rows // 8, step, 0, unroll=16)
 
 
-def tree_term(effects, growth, species, counts, noise, first_column, start, length, before):
+def tree_term(effects, growth, species, counts, noise, ids, start, length, before):
     plots, columns = effects.shape
     slots = growth.shape[1]
     block = 128
@@ -70,14 +75,14 @@
     row = lambda width: pl.BlockSpec((block, width), lambda i: (first + i, 0))
     held = [] if before is None else [before]
     return pl.pallas_call(
-        functools.partial(tree_kernel, columns // LANES),
+        functools.partial(tree_kernel, columns // LANES, first),
         grid=(length // block,),
         in_specs=[
             pl.BlockSpec(memory_space=pltpu.SMEM),
             row(columns),
             row(slots),
             row(slots),
-            row(1),
+            pl.BlockSpec(memory_space=pltpu.SMEM),
             pl.BlockSpec((1, columns), lambda i: (0, 0)),
         ]
         + [pl.BlockSpec(memory_space=pl.ANY)] * len(held),
@@ -87,8 +92,9 @@
         cost_estimate=pl.CostEstimate(
             flops=2 * length * slots * 64 * 128, bytes_accessed=8 * length * (slots + columns), transcendentals=0
         ),
+        compiler_params=pltpu.CompilerParams(vmem_limit_bytes=8 << 20),
         name="tree_term",
-    )(first_column.reshape(1), effects, growth, species, counts.reshape(plots, 1), noise.reshape(1, columns), *held)
+    )(ids, effects, growth, species, counts, noise.reshape(1, columns), *held)
 
 
 def k_row(above, centre, below, kappa):
@@ -106,8 +112,9 @@
     else:
         x_ref, top_ref, bottom_ref, kappa_ref, low_ref = refs
         get = lambda r: top_ref[0] if r == 0 else bottom_ref[0] if r == rows - 1 else x_ref[r - 1]
+    kappa = kappa_ref[...].T
     for r in range(1, rows - 1):
-        value = k_row(get(r - 1), get(r), get(r + 1), kappa_ref[r])
+        value = k_row(get(r - 1), get(r), get(r + 1), kappa[:, r : r + 1])
         low_ref[r - 1] = value.astype(low_ref.dtype)
         if with_wide:
             wide_ref[r - 1] = value
@@ -115,8 +122,9 @@
 
 def edge_kernel(with_wide, above_ref, first_ref, second_ref, before_ref, last_ref, below_ref, kappa_ref, *outs):
     rows = kappa_ref.shape[0]
-    top = k_row(above_ref[0], first_ref[0], second_ref[0], kappa_ref[0])
-    bottom = k_row(before_ref[0], last_ref[0], below_ref[0], kappa_ref[rows - 1])
+    kappa = kappa_ref[...].T
+    top = k_row(above_ref[0], first_ref[0], second_ref[0], kappa[:, :1])
+    bottom = k_row(before_ref[0], last_ref[0], below_ref[0], kappa[:, rows - 1 :])
     for at, value in enumerate((top, bottom)):
         outs[0][at] = value.astype(outs[0].dtype)
         if with_wide:
@@ -128,7 +136,7 @@
 
 
 def stencil_mid(x, edges, kappa, with_wide):
-    rows, cols = kappa.shape[:2]
+    rows, cols = kappa.shape
     columns = x.shape[2]
     shape = (rows - 2, cols, columns)
     outs = [jax.ShapeDtypeStruct(shape, jnp.bfloat16)]
@@ -138,16 +146,17 @@
     return pl.pallas_call(
         functools.partial(mid_kernel, rows, with_wide),
         grid=(columns // LANES,),
-        in_specs=[rows_spec(a.shape[0], cols) for a in arrays] + [pl.BlockSpec((rows, cols, 1), lambda j: (0, 0, 0))],
+        in_specs=[rows_spec(a.shape[0], cols) for a in arrays] + [pl.BlockSpec((rows, cols), lambda j: (0, 0))],
         out_specs=[rows_spec(rows - 2, cols) for _ in outs],
         out_shape=outs,
         cost_estimate=pl.CostEstimate(flops=8 * x.size, bytes_accessed=10 * x.size, transcendentals=0),
+        compiler_params=pltpu.CompilerParams(vmem_limit_bytes=10 << 20),
         name="stencil_mid",
     )(*arrays, kappa)
 
 
 def stencil_edge(above, first, second, before, last, below, kappa, with_wide):
-    rows, cols = kappa.shape[:2]
+    rows, cols = kappa.shape
     columns = above.shape[2]
     outs = [jax.ShapeDtypeStruct((2, cols, columns), jnp.bfloat16)]
     if with_wide:
@@ -156,10 +165,11 @@
     return pl.pallas_call(
         functools.partial(edge_kernel, with_wide),
         grid=(columns // LANES,),
-        in_specs=[rows_spec(1, cols, at) for _, at in picks] + [pl.BlockSpec((rows, cols, 1), lambda j: (0, 0, 0))],
+        in_specs=[rows_spec(1, cols, at) for _, at in picks] + [pl.BlockSpec((rows, cols), lambda j: (0, 0))],
         out_specs=[rows_spec(out.shape[0], cols) for out in outs],
         out_shape=outs,
         cost_estimate=pl.CostEstimate(flops=16 * above.size, bytes_accessed=36 * above.size, transcendentals=0),
+        compiler_params=pltpu.CompilerParams(vmem_limit_bytes=10 << 20),
         name="stencil_edge",
     )(*[array for array, _ in picks], kappa)
 
@@ -183,7 +193,7 @@
     return [pieces[d] for d in range(count)]
 
 
-def prior_kernel(pieces, *refs):
+def prior_kernel(pieces, ids_ref, *refs):
     tree_ref, out_ref = refs[2 * pieces], refs[2 * pieces + 1]
     total = None
     for at in range(pieces):
@@ -192,52 +202,64 @@
     out_ref[...] = tree_ref[...] - total
 
 
-def minus_prior(tree, pieces, weights, row_of, block):
+def minus_prior(tree, pieces, precision, ids, row_of, block):
     plots, columns = pieces[0].shape
     count = len(pieces)
-    held = pl.BlockSpec((block, columns), lambda i: (row_of(i), 0))
+    held = pl.BlockSpec((block, columns), lambda i, ids: (row_of(i), 0))
+    weight = lambda d: pl.BlockSpec((columns, columns), lambda i, ids: (ids[0] ^ d, 0))
     return pl.pallas_call(
         functools.partial(prior_kernel, count),
-        grid=(plots // block,),
-        in_specs=[pl.BlockSpec((block, columns), lambda i: (i, 0))] * count
-        + [pl.BlockSpec((columns, columns), lambda i: (0, 0))] * count
-        + [held],
-        out_specs=held,
+        grid_spec=pltpu.PrefetchScalarGridSpec(
+            num_scalar_prefetch=1,
+            grid=(plots // block,),
+            in_specs=[pl.BlockSpec((block, columns), lambda i, ids: (i, 0))] * count
+            + [weight(d) for d in range(count)]
+            + [held],
+            out_specs=held,
+        ),
         out_shape=jax.ShapeDtypeStruct(tree.shape, tree.dtype),
-        input_output_aliases={2 * count: 0},
+        input_output_aliases={2 * count + 1: 0},
         cost_estimate=pl.CostEstimate(
             flops=2 * count * plots * columns * columns, bytes_accessed=16 * plots * columns, transcendentals=0
         ),
+        compiler_params=pltpu.CompilerParams(vmem_limit_bytes=16 << 20),
         name="prior",
-    )(*pieces, *weights, tree)
-
-
-def sum_over_space(blocks, scale):
-    _, block_rows, columns = blocks.shape
-    count = lax.axis_size("space")
-    outer = count // 2
-    per_piece = count // lax.axis_size("species")
-    me, mine = lax.axis_index("space"), lax.axis_index("species")
+    )(ids, *pieces, *([precision] * count), tree)
+
+
+def pick_kernel(split, ids_ref, blocks_ref, *outs):
+    slots = blocks_ref.shape[0]
+    outer = slots // 2
+    mine, me, per_piece = ids_ref[0], ids_ref[1], ids_ref[2]
+    near_send, near_own, far_own, far_sends = outs[0], outs[1], outs[2], outs[3:]
+    for a in range(outer):
+        for b in range(2):
+            target = me ^ (2 * a + b)
+            slot = ((target // per_piece) ^ mine) * per_piece + target % per_piece
+            (near_send if b else near_own)[a] = blocks_ref[slot, :split]
+            (far_sends[a - 1] if a else far_own)[b] = blocks_ref[slot, split:]
+
+
+def sum_over_space(blocks, scale, ids):
+    slots, block_rows, columns = blocks.shape
+    outer = slots // 2
     split = max(16, block_rows * 11 // 16 // 16 * 16)
-
-    def block(target, low, high):
-        slot = ((target // per_piece) ^ mine) * per_piece + target % per_piece
-        return lax.dynamic_slice(blocks, (slot, low, 0), (1, high - low, columns))
-
-    def pair(low, high, a, b):
-        return block(me ^ (2 * a + b), low, high)
-
+    shape = lambda count, rows: jax.ShapeDtypeStruct((count, rows, columns), blocks.dtype)
+    near_send, near_own, far_own, *far_send = pl.pallas_call(
+        functools.partial(pick_kernel, split),
+        in_specs=[pl.BlockSpec(memory_space=pltpu.SMEM), pl.BlockSpec(memory_space=pltpu.VMEM)],
+        out_shape=[shape(outer, split)] * 2 + [shape(2, block_rows - split)] * outer,
+        cost_estimate=pl.CostEstimate(flops=0, bytes_accessed=4 * blocks.size, transcendentals=0),
+        compiler_params=pltpu.CompilerParams(vmem_limit_bytes=10 << 20),
+        name="pick",
+    )(ids, blocks)
     wide = lambda value: value.astype(jnp.float32)
-    near_send = jnp.concatenate([pair(0, split, a, 1) for a in range(outer)], axis=0)
     near = xor_swap(near_send, "space", 1)
-    far_send = [
-        jnp.concatenate([pair(split, block_rows, a, b) for b in range(2)], axis=0) for a in range(1, outer)
-    ]
     far = [xor_swap(far_send[a - 1], "space", 2 * a) for a in range(1, outer)]
-    near_sum = [wide(pair(0, split, a, 0)[0]) + wide(near[a]) for a in range(outer)]
+    near_sum = [wide(near_own[a]) + wide(near[a]) for a in range(outer)]
     near_low = [value.astype(jnp.bfloat16) for value in near_sum]
     near_far = [xor_swap(near_low[a], "space", 2 * a) for a in range(1, outer)]
-    far_sum = [wide(pair(split, block_rows, 0, b)[0]) for b in range(2)]
+    far_sum = [wide(far_own[b]) for b in range(2)]
     for part in far:
         far_sum = [far_sum[b] + wide(part[b]) for b in range(2)]
     far_near = xor_swap(far_sum[1].astype(jnp.bfloat16), "space", 1)
@@ -255,7 +277,9 @@
     space_count = lax.axis_size("space")
     species_count = lax.axis_size("species")
     mine = lax.axis_index("species")
-    kappa = kappa_sq.reshape(rows, cols, 1)
+    kappa = kappa_sq
+    ids = jnp.stack([mine, lax.axis_index("space"), jnp.int32(space_count // species_count), mine * columns])
+    effects, ids = lax.optimization_barrier((effects, ids))
     flat = lambda value: value.reshape(-1, columns)
     above, below = halo(effects[:1], effects[rows - 1 :])
     mid_low, mid_wide = stencil_mid(effects, [], kappa, True)
@@ -269,9 +293,9 @@
             effects.reshape(plots, columns),
             growth.reshape(plots, slots),
             tree_species.reshape(plots, slots),
-            tree_counts.reshape(plots),
+            tree_counts,
             noise_precision,
-            mine * columns,
+            ids,
             at * length,
             length,
             before,
@@ -297,18 +321,14 @@
         part = product(mid_pieces[d], mid_pieces[0]) + product(edge_pieces[d], edge_pieces[0])
         grams.append(part.astype(jnp.bfloat16))
     blocks = jnp.stack(grams).reshape(space_count, -1, columns)
-    gram = sum_over_space(blocks, -0.5 / (plots * space_count))
+    gram = sum_over_space(blocks, -0.5 / (plots * space_count), ids)
 
     (spatial_edge,) = stencil_edge(
         above_k, (top_wide, 0), (mid_wide, 0), (mid_wide, rows - 3), (bottom_wide, 0), below_k, kappa, False
     )
     spatial_edge_pieces = gather_pieces(flat(spatial_edge))
-    weights = [
-        lax.dynamic_slice(species_precision, ((mine ^ d) * columns, 0), (columns, columns))
-        for d in range(species_count)
-    ]
-    grad = minus_prior(tree, spatial_mid_pieces, weights, lambda i: i + 1, cols)
-    grad = minus_prior(grad, spatial_edge_pieces, weights, lambda i: i * (rows - 1), cols)
+    grad = minus_prior(tree, spatial_mid_pieces, species_precision, ids, lambda i: i + 1, cols)
+    grad = minus_prior(grad, spatial_edge_pieces, species_precision, ids, lambda i: i * (rows - 1), cols)
     return (grad.reshape(rows, cols, columns), gram)
 
 

time: 149 us -> 129 us (0.87)
  Pallas kernels: 54.7 us -> 39.1 us
  starting transfers between devices: 33.3 us -> 40.1 us
  other arithmetic: 7.09 us -> 1.54 us
  local copies, waits for them, and re-layouts: 7.48 us -> 3.18 us
  matrix products: 9.08 us -> 4.79 us
  waiting for transfers between devices: 34.8 us -> 38.1 us
    ppermute x20, starting transfers between devices: 20.5 us -> 28.1 us  [xor_swap(): return lax.ppermute(value, axis, [(i, i ^ mask) for i in range(count)])]
    ppermute x2, waiting for transfers between devices: 8.21 us -> 15.2 us  [halo(): above = lax.ppermute(last, 'space', forward)]
    pallas_call x2, Pallas kernels: 8.94 us -> 3.66 us  [stencil_edge(): pl.pallas_call(functools.partial(edge_kernel, with_wide), grid=(columns /...]
    pallas_call x5 -> x6, Pallas kernels: 36.1 us -> 30.8 us  [the longest x3 20.5 us: tree_term(): pl.pallas_call(functools.partial(tree_kernel, columns // LANES, first), g...]
    pallas_call x2, Pallas kernels: 9.7 us -> 4.68 us  [stencil_mid(): pl.pallas_call(functools.partial(mid_kernel, rows, with_wide), grid=(colu...]
    dot_general x8, matrix products: 9.08 us -> 4.79 us  [product(): lax.dot_general(left, right, (((0,), (0,)), ((), ())), preferred_element_...]
    ppermute x20, waiting for transfers between devices: 26.6 us -> 23 us  [xor_swap(): return lax.ppermute(value, axis, [(i, i ^ mask) for i in range(count)])]
    convert_element_type x1, other arithmetic: 1.99 us -> 0.14 us  [sum_over_space(): near_low = [value.astype(jnp.bfloat16) for value in near_sum]]
  transfers between devices with their start and end apart: 24 -> 24, of which waited for: 8 -> 4; matrix products, arithmetic and copies ran while one was open for 13% -> 4% of each run, Pallas kernels for 37% -> 31%
where the time goes in v2:
time: 129 us; the launch traced here: 128 us
  starting transfers between devices  40.1 us (31%)
  Pallas kernels  39.1 us (30%)
  waiting for transfers between devices  38.1 us (30%)
  matrix products  4.79 us (4%)
  local copies, waits for them, and re-layouts  3.18 us (2%)
  other arithmetic  1.54 us (1%)
    ppermute x20, starting transfers between devices, xor_swap(): return lax.ppermute(value, axis, [(i, i ^ mask) for i in range(count)])  28.1 us
    ppermute x20, waiting for transfers between devices, xor_swap(): return lax.ppermute(value, axis, [(i, i ^ mask) for i in range(count)])  23 us
    pallas_call x3, Pallas kernels, tree_term(): pl.pallas_call(functools.partial(tree_kernel, columns // LANES, first), g...  20.5 us
    ppermute x2, waiting for transfers between devices, halo(): above = lax.ppermute(last, 'space', forward)  15.2 us
    pallas_call x2, Pallas kernels, minus_prior(): pl.pallas_call(functools.partial(prior_kernel, count), grid_spec=pltpu.Pr...  9.64 us
    ppermute x2, starting transfers between devices, halo(): above = lax.ppermute(last, 'space', forward)  9.34 us
    dot_general x8, matrix products, product(): lax.dot_general(left, right, (((0,), (0,)), ((), ())), preferred_element_...  4.79 us
    pallas_call x2, Pallas kernels, stencil_mid(): pl.pallas_call(functools.partial(mid_kernel, rows, with_wide), grid=(colu...  4.68 us
  transfers between devices with their start and end apart: 24, of which 4 were waited for; matrix products, arithmetic and copies ran while one was open for 4% of the time, Pallas kernels for 31%

profile of v2, /device:TPU:0, one launch (start us, length us, event | category | flops | bytes accessed | tf_op | source)
XLA Modules:
  0.0 127.8 jit_solution(14159491921287423702)
XLA Ops:
  0.6 0.1 pad_add_fusion.first_ref.ids_ref
  0.7 1.3 fusion.15
  2.0 4.9 %collective-permute-start = (f32[1,256,512]{2,1,0:T(8,128)S(1)}, f32[1,256,512]{2,1,0:T(8,128)S(1)}, u32[]{:S(2)}, u32[]{:S(2)}) collective-permute-start(f32[1,256,512]{2,1,0:T(8,128)S(1)} %get-tuple-element.29), channel_id=1, source_target_pairs={{0,4},{4,8},{8,12},{12,16},{16,20},{20,24},{24,28},{1,5},{5,9},{9,... | collective-permute-start | bytes 1572872 | tf_op jit(solution)/shard_map/ppermute | solution.py:181
  6.9 1.3 %collective-permute-start.1 = (f32[1,256,512]{2,1,0:T(8,128)S(1)}, f32[1,256,512]{2,1,0:T(8,128)S(1)}, u32[]{:S(2)}, u32[]{:S(2)}) collective-permute-start(f32[1,256,512]{2,1,0:T(8,128)S(1)} %get-tuple-element.28), channel_id=1, source_target_pairs={{4,0},{8,4},{12,8},{16,12},{20,16},{24,20},{28,24},{5,1},{9,5},{13... | collective-permute-start | bytes 1572872 | tf_op jit(solution)/shard_map/ppermute | solution.py:182
  8.3 1.9 %copy-done = f32[6,256,512]{2,1,0:T(8,128)S(1)} copy-done((f32[6,256,512]{2,1,0:T(8,128)S(1)}, f32[6,256,512]{2,1,0:T(8,128)}, u32[]{:S(2)}) %copy-start) | copy-done | bytes 3145752
  10.1 2.4 %stencil_mid.2 = (bf16[4,256,512]{2,1,0:T(8,128)(2,1)S(1)}, f32[4,256,512]{2,1,0:T(8,128)S(1)}) custom-call(f32[6,256,512]{2,1,0:T(8,128)S(1)} %copy-done, f32[6,256]{1,0:T(8,128)S(1)} %copy-done.5), custom_call_target="tpu_custom_call" | custom-call | flops 6291456 | bytes 7864320 | tf_op jit(solution)/shard_map/stencil_mid/pallas_call | solution.py:146
  12.6 1.6 %collective-permute-start.12 = (bf16[1024,512]{1,0:T(8,128)(2,1)S(1)}, bf16[1024,512]{1,0:T(8,128)(2,1)S(1)}, u32[]{:S(2)}, u32[]{:S(2)}) collective-permute-start(bf16[1024,512]{1,0:T(8,128)(2,1)S(1)} %bitcast.87), channel_id=1, source_target_pairs={{0,2},{1,3},{2,0},{3,1},{4,6},{5,7},{6,4},{7,5},{8,10},{9,11},{10,... | collective-permute-start | bytes 3145736 | tf_op jit(solution)/shard_map/ppermute | solution.py:16
  14.2 15.2 %collective-permute-done.above_ref = f32[1,256,512]{2,1,0:T(8,128)S(1)} collective-permute-done((f32[1,256,512]{2,1,0:T(8,128)S(1)}, f32[1,256,512]{2,1,0:T(8,128)S(1)}, u32[]{:S(2)}, u32[]{:S(2)}) %collective-permute-start) | collective-permute-done | bytes 524320 | tf_op jit(solution)/shard_map/ppermute | solution.py:181
  29.3 1.9 %stencil_edge.2 = (bf16[2,256,512]{2,1,0:T(8,128)(2,1)S(1)}, f32[1,256,512]{2,1,0:T(8,128)S(1)}, f32[1,256,512]{2,1,0:T(8,128)S(1)}) custom-call(f32[1,256,512]{2,1,0:T(8,128)S(1)} %collective-permute-done.above_ref, f32[6,256,512]{2,1,0:T(8,128)S(1)} %copy-done.1, f32[6,256,512]{2,1,0:T(8,128)S(1)} %copy-done.1, f32[6,256,512]{2,1,0:T(8,128)S(1)} %copy-done.1, ...), custom_call_target="tpu_custom_call" | custom-call | flops 2097152 | bytes 4718592 | tf_op jit(solution)/shard_map/stencil_edge/pallas_call | solution.py:165
  31.2 1.6 %collective-permute-start.13 = (bf16[512,512]{1,0:T(8,128)(2,1)S(1)}, bf16[512,512]{1,0:T(8,128)(2,1)S(1)}, u32[]{:S(2)}, u32[]{:S(2)}) collective-permute-start(bf16[512,512]{1,0:T(8,128)(2,1)S(1)} %bitcast.66), channel_id=1, source_target_pairs={{0,2},{1,3},{2,0},{3,1},{4,6},{5,7},{6,4},{7,5},{8,10},{9,11},{10,... | collective-permute-start | bytes 1572872 | tf_op jit(solution)/shard_map/ppermute | solution.py:16
  32.8 0.7 convolution_bitcast_fusion.1
  33.5 0.6 collective-permute-start.11
  34.1 4.4 %collective-permute-start.2 = (f32[1,256,512]{2,1,0:T(8,128)S(1)}, f32[1,256,512]{2,1,0:T(8,128)S(1)}, u32[]{:S(2)}, u32[]{:S(2)}) collective-permute-start(f32[1,256,512]{2,1,0:T(8,128)S(1)} %get-tuple-element.17.last_ref.refs_2_), channel_id=1, source_target_pairs={{0,4},{4,8},{8,12},{12,16},{16,20},{20,24},{24,28},{1,5},{5,9},{9,... | collective-permute-start | bytes 1572872 | tf_op jit(solution)/shard_map/ppermute | solution.py:181
  38.5 2.2 %stencil_mid.3 = bf16[4,256,512]{2,1,0:T(8,128)(2,1)S(1)} custom-call(f32[4,256,512]{2,1,0:T(8,128)S(1)} %get-tuple-element.19.second_ref.before_ref.refs_0_, f32[1,256,512]{2,1,0:T(8,128)S(1)} %get-tuple-element.18.first_ref.refs_1_, f32[1,256,512]{2,1,0:T(8,128)S(1)} %get-tuple-element.17.last_ref.refs_2_, f32[6,256]{1,0:T(8,128)S(1)} %copy-done.5), custom_call_target="tpu_custom_call" | custom-call | flops 4194304 | bytes 5242880 | tf_op jit(solution)/shard_map/stencil_mid/pallas_call | solution.py:146
  40.7 0.5 fusion.5
  41.2 7.3 %collective-permute-done.13 = bf16[512,512]{1,0:T(8,128)(2,1)S(1)} collective-permute-done((bf16[512,512]{1,0:T(8,128)(2,1)S(1)}, bf16[512,512]{1,0:T(8,128)(2,1)S(1)}, u32[]{:S(2)}, u32[]{:S(2)}) %collective-permute-start.13) | collective-permute-done | bytes 524320 | tf_op jit(solution)/shard_map/ppermute | solution.py:16
  48.5 1.5 %collective-permute-start.3 = (f32[1,256,512]{2,1,0:T(8,128)S(1)}, f32[1,256,512]{2,1,0:T(8,128)S(1)}, u32[]{:S(2)}, u32[]{:S(2)}) collective-permute-start(f32[1,256,512]{2,1,0:T(8,128)S(1)} %get-tuple-element.18.first_ref.refs_1_), channel_id=1, source_target_pairs={{4,0},{8,4},{12,8},{16,12},{20,16},{24,20},{28,24},{5,1},{9,5},{13... | collective-permute-start | bytes 1572872 | tf_op jit(solution)/shard_map/ppermute | solution.py:182
  50.0 0.1 collective-permute-start.14
  50.1 0.5 fusion.17
  50.5 0.7 fusion.7
  51.3 0.6 collective-permute-start.15
  51.8 0.5 fusion.16
  52.3 1.6 %collective-permute-start.8 = (bf16[1024,512]{1,0:T(8,128)(2,1)S(1)}, bf16[1024,512]{1,0:T(8,128)(2,1)S(1)}, u32[]{:S(2)}, u32[]{:S(2)}) collective-permute-start(bf16[1024,512]{1,0:T(8,128)(2,1)S(1)} %bitcast.78), channel_id=1, source_target_pairs={{0,2},{1,3},{2,0},{3,1},{4,6},{5,7},{6,4},{7,5},{8,10},{9,11},{10,... | collective-permute-start | bytes 3145736 | tf_op jit(solution)/shard_map/ppermute | solution.py:16
  53.9 0.7 fusion.8
  54.6 0.5 fusion.18
  55.1 0.7 fusion.6
  55.8 0.3 pad_maximum_fusion
  56.1 0.7 pick.1
  56.8 4.5 %collective-permute-start.20 = (bf16[2,80,512]{2,1,0:T(8,128)(2,1)S(1)}, bf16[2,80,512]{2,1,0:T(8,128)(2,1)S(1)}, u32[]{:S(2)}, u32[]{:S(2)}) collective-permute-start(bf16[2,80,512]{2,1,0:T(8,128)(2,1)S(1)} %get-tuple-element.25), channel_id=1, source_target_pairs={{0,8},{4,12},{8,0},{12,4},{16,24},{20,28},{24,16},{28,20},{1,9},{5... | collective-permute-start | bytes 491528 | tf_op jit(solution)/shard_map/ppermute | solution.py:16
  61.3 2.6 %collective-permute-start.21 = (bf16[2,80,512]{2,1,0:T(8,128)(2,1)S(1)}, bf16[2,80,512]{2,1,0:T(8,128)(2,1)S(1)}, u32[]{:S(2)}, u32[]{:S(2)}) collective-permute-start(bf16[2,80,512]{2,1,0:T(8,128)(2,1)S(1)} %get-tuple-element.26), channel_id=1, source_target_pairs={{0,16},{4,20},{8,24},{12,28},{16,0},{20,4},{24,8},{28,12},{1,17},{... | collective-permute-start | bytes 491528 | tf_op jit(solution)/shard_map/ppermute | solution.py:16
  64.0 13.5 %collective-permute-done.8.refs_2_ = bf16[1024,512]{1,0:T(8,128)(2,1)S(1)} collective-permute-done((bf16[1024,512]{1,0:T(8,128)(2,1)S(1)}, bf16[1024,512]{1,0:T(8,128)(2,1)S(1)}, u32[]{:S(2)}, u32[]{:S(2)}) %collective-permute-start.8) | collective-permute-done | bytes 1048608 | tf_op jit(solution)/shard_map/ppermute | solution.py:16
  77.5 1.8 %stencil_edge.3 = bf16[2,256,512]{2,1,0:T(8,128)(2,1)S(1)} custom-call(f32[1,256,512]{2,1,0:T(8,128)S(1)} %collective-permute-done.2.above_ref, f32[1,256,512]{2,1,0:T(8,128)S(1)} %get-tuple-element.18.first_ref.refs_1_, f32[4,256,512]{2,1,0:T(8,128)S(1)} %get-tuple-element.19.second_ref.before_ref.refs_0_, ...), custom_call_target="tpu_custom_call" | custom-call | flops 2097152 | bytes 4718592 | tf_op jit(solution)/shard_map/stencil_edge/pallas_call | solution.py:165
  79.3 1.6 %collective-permute-start.5 = (bf16[512,512]{1,0:T(8,128)(2,1)S(1)}, bf16[512,512]{1,0:T(8,128)(2,1)S(1)}, u32[]{:S(2)}, u32[]{:S(2)}) collective-permute-start(bf16[512,512]{1,0:T(8,128)(2,1)S(1)} %bitcast.81), channel_id=1, source_target_pairs={{0,2},{1,3},{2,0},{3,1},{4,6},{5,7},{6,4},{7,5},{8,10},{9,11},{10,... | collective-permute-start | bytes 1572872 | tf_op jit(solution)/shard_map/ppermute | solution.py:16
  80.8 3.0 %collective-permute-start.16 = (bf16[4,176,512]{2,1,0:T(8,128)(2,1)S(1)}, bf16[4,176,512]{2,1,0:T(8,128)(2,1)S(1)}, u32[]{:S(2)}, u32[]{:S(2)}) collective-permute-start(bf16[4,176,512]{2,1,0:T(8,128)(2,1)S(1)} %get-tuple-element.23), channel_id=1, source_target_pairs={{0,4},{4,0},{8,12},{12,8},{16,20},{20,16},{24,28},{28,24},{1,5},{5... | collective-permute-start | bytes 2162696 | tf_op jit(solution)/shard_map/ppermute | solution.py:16
  83.8 5.0 %collective-permute-start.22 = (bf16[2,80,512]{2,1,0:T(8,128)(2,1)S(1)}, bf16[2,80,512]{2,1,0:T(8,128)(2,1)S(1)}, u32[]{:S(2)}, u32[]{:S(2)}) collective-permute-start(bf16[2,80,512]{2,1,0:T(8,128)(2,1)S(1)} %get-tuple-element.27), channel_id=1, source_target_pairs={{0,24},{4,28},{8,16},{12,20},{16,8},{20,12},{24,0},{28,4},{1,25},{... | collective-permute-start | bytes 491528 | tf_op jit(solution)/shard_map/ppermute | solution.py:16
  88.8 6.8 %tree_term.3.rest_0_ = f32[1536,512]{1,0:T(8,128)} custom-call(s32[4]{0:T(128)S(1)} %pad_add_fusion.first_ref.ids_ref, f32[1536,512]{1,0:T(8,128)S(1)} %bitcast.63, f32[1536,128]{1,0:T(8,128)S(1)} %bitcast.72, s32[1536,128]{1,0:T(8,128)S(1)} %bitcast.75, s32[6,256]{1,0:T(8,128)S(1)} %copy-done.6, f32[1,512]{1,0:T(1,128)S(1)} %bitcast.84), custom_call_target="tpu_custom_call" | custom-call | flops 1073741824 | bytes 2621440 | tf_op jit(solution)/shard_map/tree_term/pallas_call | solution.py:77
  95.7 6.8 %tree_term.4.rest_0_ = f32[1536,512]{1,0:T(8,128)} custom-call(s32[4]{0:T(128)S(1)} %pad_add_fusion.first_ref.ids_ref, f32[1536,512]{1,0:T(8,128)S(1)} %bitcast.64, f32[1536,128]{1,0:T(8,128)S(1)} %bitcast.73, s32[1536,128]{1,0:T(8,128)S(1)} %bitcast.76, s32[6,256]{1,0:T(8,128)S(1)} %copy-done.6, ...), custom_call_target="tpu_custom_call", output_to_operand_aliasing={{}: (6, {})} | custom-call | flops 1073741824 | bytes 2621440 | tf_op jit(solution)/shard_map/tree_term/pallas_call | solution.py:77
  102.5 0.6 collective-permute-start.23
  103.1 6.8 %tree_term.5.refs_8_ = f32[1536,512]{1,0:T(8,128)} custom-call(s32[4]{0:T(128)S(1)} %pad_add_fusion.first_ref.ids_ref, f32[1536,512]{1,0:T(8,128)S(1)} %bitcast.65, f32[1536,128]{1,0:T(8,128)S(1)} %bitcast.74, s32[1536,128]{1,0:T(8,128)S(1)} %bitcast.77, s32[6,256]{1,0:T(8,128)S(1)} %copy-done.6, ...), custom_call_target="tpu_custom_call", output_to_operand_aliasing={{}: (6, {})} | custom-call | flops 1073741824 | bytes 2621440 | tf_op jit(solution)/shard_map/tree_term/pallas_call | solution.py:77
  109.9 0.5 collective-permute-start.6
  110.5 0.1 fusion.11
  110.7 0.6 collective-permute-start.18
  111.3 3.8 %collective-permute-start.19 = (bf16[176,512]{1,0:T(8,128)(2,1)S(1)}, bf16[176,512]{1,0:T(8,128)(2,1)S(1)}, u32[]{:S(2)}, u32[]{:S(2)}) collective-permute-start(bf16[176,512]{1,0:T(8,128)(2,1)S(1)} %get-tuple-element.31), channel_id=1, source_target_pairs={{0,24},{4,28},{8,16},{12,20},{16,8},{20,12},{24,0},{28,4},{1,25},{... | collective-permute-start | bytes 540680 | tf_op jit(solution)/shard_map/ppermute | solution.py:16
  115.1 5.8 %prior.2.refs_8_ = f32[1536,512]{1,0:T(8,128)} custom-call(s32[4]{0:T(128)S(1)} %pad_add_fusion.first_ref.ids_ref, bf16[1024,512]{1,0:T(8,128)(2,1)S(1)} %bitcast.80, bf16[1024,512]{1,0:T(8,128)(2,1)S(1)} %collective-permute-done.7.refs_1_, bf16[1024,512]{1,0:T(8,128)(2,1)S(1)} %collective-permute-done.8.refs_2_, ...), custom_call_target="tpu_custom_call", output_to_operand_aliasing={{}: (9, {})} | custom-call | flops 2147483648 | bytes 8388608 | tf_op jit(solution)/shard_map/prior/pallas_call | solution.py:210
  120.9 3.8 %prior.3 = f32[1536,512]{1,0:T(8,128)} custom-call(s32[4]{0:T(128)S(1)} %pad_add_fusion.first_ref.ids_ref, bf16[512,512]{1,0:T(8,128)(2,1)S(1)} %bitcast.83, bf16[512,512]{1,0:T(8,128)(2,1)S(1)} %collective-permute-done.4.refs_1_, bf16[512,512]{1,0:T(8,128)(2,1)S(1)} %collective-permute-done.5.refs_2_, ...), custom_call_target="tpu_custom_call", output_to_operand_aliasing={{}: (9, {})} | custom-call | flops 1073741824 | bytes 4194304 | tf_op jit(solution)/shard_map/prior/pallas_call | solution.py:210
  124.7 2.1 %collective-permute-done.18 = bf16[176,512]{1,0:T(8,128)(2,1)S(1)} collective-permute-done((bf16[176,512]{1,0:T(8,128)(2,1)S(1)}, bf16[176,512]{1,0:T(8,128)(2,1)S(1)}, u32[]{:S(2)}, u32[]{:S(2)}) %collective-permute-start.18) | collective-permute-done | bytes 180256 | tf_op jit(solution)/shard_map/ppermute | solution.py:16
  126.9 0.1 fusion.10
  127.0 0.9 maximum_multiply_fusion
  (42 shorter events, 0.3 us)
Async XLA Ops:
  0.6 7.6 %copy-start.5 = (f32[6,256]{1,0:T(8,128)S(1)}, f32[6,256]{1,0:T(8,128)}, u32[]{:S(2)}) copy-start(f32[6,256]{1,0:T(8,128)} %refs_3_.1) | copy-start | bytes 18436
  2.0 27.3 %collective-permute-start = (f32[1,256,512]{2,1,0:T(8,128)S(1)}, f32[1,256,512]{2,1,0:T(8,128)S(1)}, u32[]{:S(2)}, u32[]{:S(2)}) collective-permute-start(f32[1,256,512]{2,1,0:T(8,128)S(1)} %get-tuple-element.29), channel_id=1, source_target_pairs={{0,4},{4,8},{8,12},{12,16},{16,20},{20,24},{24,28},{1,5},{5,9},{9,... | collective-permute-start | bytes 1572872 | tf_op jit(solution)/shard_map/ppermute | solution.py:181
  6.9 22.4 %collective-permute-start.1 = (f32[1,256,512]{2,1,0:T(8,128)S(1)}, f32[1,256,512]{2,1,0:T(8,128)S(1)}, u32[]{:S(2)}, u32[]{:S(2)}) collective-permute-start(f32[1,256,512]{2,1,0:T(8,128)S(1)} %get-tuple-element.28), channel_id=1, source_target_pairs={{4,0},{8,4},{12,8},{16,12},{20,16},{24,20},{28,24},{5,1},{9,5},{13... | collective-permute-start | bytes 1572872 | tf_op jit(solution)/shard_map/ppermute | solution.py:182
  8.2 1.9 %copy-start = (f32[6,256,512]{2,1,0:T(8,128)S(1)}, f32[6,256,512]{2,1,0:T(8,128)}, u32[]{:S(2)}) copy-start(f32[6,256,512]{2,1,0:T(8,128)} %refs_0_) | copy-start | bytes 9437188
  10.1 19.2 %copy-start.1 = (f32[6,256,512]{2,1,0:T(8,128)S(1)}, f32[6,256,512]{2,1,0:T(8,128)}, u32[]{:S(2)}) copy-start(f32[6,256,512]{2,1,0:T(8,128)} %refs_0_) | copy-start | bytes 9437188
  12.6 37.4 %collective-permute-start.12 = (bf16[1024,512]{1,0:T(8,128)(2,1)S(1)}, bf16[1024,512]{1,0:T(8,128)(2,1)S(1)}, u32[]{:S(2)}, u32[]{:S(2)}) collective-permute-start(bf16[1024,512]{1,0:T(8,128)(2,1)S(1)} %bitcast.87), channel_id=1, source_target_pairs={{0,2},{1,3},{2,0},{3,1},{4,6},{5,7},{6,4},{7,5},{8,10},{9,11},{10,... | collective-permute-start | bytes 3145736 | tf_op jit(solution)/shard_map/ppermute | solution.py:16
  31.2 17.3 %collective-permute-start.13 = (bf16[512,512]{1,0:T(8,128)(2,1)S(1)}, bf16[512,512]{1,0:T(8,128)(2,1)S(1)}, u32[]{:S(2)}, u32[]{:S(2)}) collective-permute-start(bf16[512,512]{1,0:T(8,128)(2,1)S(1)} %bitcast.66), channel_id=1, source_target_pairs={{0,2},{1,3},{2,0},{3,1},{4,6},{5,7},{6,4},{7,5},{8,10},{9,11},{10,... | collective-permute-start | bytes 1572872 | tf_op jit(solution)/shard_map/ppermute | solution.py:16
  32.8 19.5 %collective-permute-start.10 = (bf16[1024,512]{1,0:T(8,128)(2,1)S(1)}, bf16[1024,512]{1,0:T(8,128)(2,1)S(1)}, u32[]{:S(2)}, u32[]{:S(2)}) collective-permute-start(bf16[1024,512]{1,0:T(8,128)(2,1)S(1)} %bitcast.88), channel_id=1, source_target_pairs={{0,1},{1,0},{2,3},{3,2},{4,5},{5,4},{6,7},{7,6},{8,9},{9,8},{10,11... | collective-permute-start | bytes 3145736 | tf_op jit(solution)/shard_map/ppermute | solution.py:16
  33.5 17.8 %collective-permute-start.11 = (bf16[512,512]{1,0:T(8,128)(2,1)S(1)}, bf16[512,512]{1,0:T(8,128)(2,1)S(1)}, u32[]{:S(2)}, u32[]{:S(2)}) collective-permute-start(bf16[512,512]{1,0:T(8,128)(2,1)S(1)} %bitcast.67), channel_id=1, source_target_pairs={{0,1},{1,0},{2,3},{3,2},{4,5},{5,4},{6,7},{7,6},{8,9},{9,8},{10,11... | collective-permute-start | bytes 1572872 | tf_op jit(solution)/shard_map/ppermute | solution.py:16
  34.1 29.9 %collective-permute-start.2 = (f32[1,256,512]{2,1,0:T(8,128)S(1)}, f32[1,256,512]{2,1,0:T(8,128)S(1)}, u32[]{:S(2)}, u32[]{:S(2)}) collective-permute-start(f32[1,256,512]{2,1,0:T(8,128)S(1)} %get-tuple-element.17.last_ref.refs_2_), channel_id=1, source_target_pairs={{0,4},{4,8},{8,12},{12,16},{16,20},{20,24},{24,28},{1,5},{5,9},{9,... | collective-permute-start | bytes 1572872 | tf_op jit(solution)/shard_map/ppermute | solution.py:181
  48.5 29.0 %collective-permute-start.3 = (f32[1,256,512]{2,1,0:T(8,128)S(1)}, f32[1,256,512]{2,1,0:T(8,128)S(1)}, u32[]{:S(2)}, u32[]{:S(2)}) collective-permute-start(f32[1,256,512]{2,1,0:T(8,128)S(1)} %get-tuple-element.18.first_ref.refs_1_), channel_id=1, source_target_pairs={{4,0},{8,4},{12,8},{16,12},{20,16},{24,20},{28,24},{5,1},{9,5},{13... | collective-permute-start | bytes 1572872 | tf_op jit(solution)/shard_map/ppermute | solution.py:182
  50.0 5.1 %collective-permute-start.14 = (bf16[1024,512]{1,0:T(8,128)(2,1)S(1)}, bf16[1024,512]{1,0:T(8,128)(2,1)S(1)}, u32[]{:S(2)}, u32[]{:S(2)}) collective-permute-start(bf16[1024,512]{1,0:T(8,128)(2,1)S(1)} %collective-permute-done.12), channel_id=1, source_target_pairs={{0,1},{1,0},{2,3},{3,2},{4,5},{5,4},{6,7},{7,6},{8,9},{9,8},{10,11... | collective-permute-start | bytes 3145736 | tf_op jit(solution)/shard_map/ppermute | solution.py:16
  51.3 3.3 %collective-permute-start.15 = (bf16[512,512]{1,0:T(8,128)(2,1)S(1)}, bf16[512,512]{1,0:T(8,128)(2,1)S(1)}, u32[]{:S(2)}, u32[]{:S(2)}) collective-permute-start(bf16[512,512]{1,0:T(8,128)(2,1)S(1)} %collective-permute-done.13), channel_id=1, source_target_pairs={{0,1},{1,0},{2,3},{3,2},{4,5},{5,4},{6,7},{7,6},{8,9},{9,8},{10,11... | collective-permute-start | bytes 1572872 | tf_op jit(solution)/shard_map/ppermute | solution.py:16
  52.3 25.1 %collective-permute-start.8 = (bf16[1024,512]{1,0:T(8,128)(2,1)S(1)}, bf16[1024,512]{1,0:T(8,128)(2,1)S(1)}, u32[]{:S(2)}, u32[]{:S(2)}) collective-permute-start(bf16[1024,512]{1,0:T(8,128)(2,1)S(1)} %bitcast.78), channel_id=1, source_target_pairs={{0,2},{1,3},{2,0},{3,1},{4,6},{5,7},{6,4},{7,5},{8,10},{9,11},{10,... | collective-permute-start | bytes 3145736 | tf_op jit(solution)/shard_map/ppermute | solution.py:16
  56.8 24.0 %collective-permute-start.20 = (bf16[2,80,512]{2,1,0:T(8,128)(2,1)S(1)}, bf16[2,80,512]{2,1,0:T(8,128)(2,1)S(1)}, u32[]{:S(2)}, u32[]{:S(2)}) collective-permute-start(bf16[2,80,512]{2,1,0:T(8,128)(2,1)S(1)} %get-tuple-element.25), channel_id=1, source_target_pairs={{0,8},{4,12},{8,0},{12,4},{16,24},{20,28},{24,16},{28,20},{1,9},{5... | collective-permute-start | bytes 491528 | tf_op jit(solution)/shard_map/ppermute | solution.py:16
  61.3 27.5 %copy-start.3 = (f32[6,256,128]{2,1,0:T(8,128)S(1)}, f32[6,256,128]{2,1,0:T(8,128)}, u32[]{:S(2)}) copy-start(f32[6,256,128]{2,1,0:T(8,128)} %param.9) | copy-start | bytes 2359300
  61.3 27.5 %copy-start.4 = (s32[6,256,128]{2,1,0:T(8,128)S(1)}, s32[6,256,128]{2,1,0:T(8,128)}, u32[]{:S(2)}) copy-start(s32[6,256,128]{2,1,0:T(8,128)} %param.10) | copy-start | bytes 2359300
  61.3 27.5 %copy-start.6 = (s32[6,256]{1,0:T(8,128)S(1)}, s32[6,256]{1,0:T(8,128)}, u32[]{:S(2)}) copy-start(s32[6,256]{1,0:T(8,128)} %counts_ref.5) | copy-start | bytes 18436
  61.3 27.5 %copy-start.7 = (f32[512]{0:T(512)S(1)}, f32[512]{0:T(512)}, u32[]{:S(2)}) copy-start(f32[512]{0:T(512)} %param.12) | copy-start | bytes 6148
  61.3 22.5 %collective-permute-start.21 = (bf16[2,80,512]{2,1,0:T(8,128)(2,1)S(1)}, bf16[2,80,512]{2,1,0:T(8,128)(2,1)S(1)}, u32[]{:S(2)}, u32[]{:S(2)}) collective-permute-start(bf16[2,80,512]{2,1,0:T(8,128)(2,1)S(1)} %get-tuple-element.26), channel_id=1, source_target_pairs={{0,16},{4,20},{8,24},{12,28},{16,0},{20,4},{24,8},{28,12},{1,17},{... | collective-permute-start | bytes 491528 | tf_op jit(solution)/shard_map/ppermute | solution.py:16
  64.0 46.7 %collective-permute-start.7 = (bf16[1024,512]{1,0:T(8,128)(2,1)S(1)}, bf16[1024,512]{1,0:T(8,128)(2,1)S(1)}, u32[]{:S(2)}, u32[]{:S(2)}) collective-permute-start(bf16[1024,512]{1,0:T(8,128)(2,1)S(1)} %bitcast.79), channel_id=1, source_target_pairs={{0,1},{1,0},{2,3},{3,2},{4,5},{5,4},{6,7},{7,6},{8,9},{9,8},{10,11... | collective-permute-start | bytes 3145736 | tf_op jit(solution)/shard_map/ppermute | solution.py:16
  77.5 33.8 %collective-permute-start.9 = (bf16[1024,512]{1,0:T(8,128)(2,1)S(1)}, bf16[1024,512]{1,0:T(8,128)(2,1)S(1)}, u32[]{:S(2)}, u32[]{:S(2)}) collective-permute-start(bf16[1024,512]{1,0:T(8,128)(2,1)S(1)} %collective-permute-done.8.refs_2_), channel_id=1, source_target_pairs={{0,1},{1,0},{2,3},{3,2},{4,5},{5,4},{6,7},{7,6},{8,9},{9,8},{10,11... | collective-permute-start | bytes 3145736 | tf_op jit(solution)/shard_map/ppermute | solution.py:16
  79.3 30.6 %collective-permute-start.5 = (bf16[512,512]{1,0:T(8,128)(2,1)S(1)}, bf16[512,512]{1,0:T(8,128)(2,1)S(1)}, u32[]{:S(2)}, u32[]{:S(2)}) collective-permute-start(bf16[512,512]{1,0:T(8,128)(2,1)S(1)} %bitcast.81), channel_id=1, source_target_pairs={{0,2},{1,3},{2,0},{3,1},{4,6},{5,7},{6,4},{7,5},{8,10},{9,11},{10,... | collective-permute-start | bytes 1572872 | tf_op jit(solution)/shard_map/ppermute | solution.py:16
  80.8 29.6 %collective-permute-start.16 = (bf16[4,176,512]{2,1,0:T(8,128)(2,1)S(1)}, bf16[4,176,512]{2,1,0:T(8,128)(2,1)S(1)}, u32[]{:S(2)}, u32[]{:S(2)}) collective-permute-start(bf16[4,176,512]{2,1,0:T(8,128)(2,1)S(1)} %get-tuple-element.23), channel_id=1, source_target_pairs={{0,4},{4,0},{8,12},{12,8},{16,20},{20,16},{24,28},{28,24},{1,5},{5... | collective-permute-start | bytes 2162696 | tf_op jit(solution)/shard_map/ppermute | solution.py:16
  83.8 18.7 %collective-permute-start.22 = (bf16[2,80,512]{2,1,0:T(8,128)(2,1)S(1)}, bf16[2,80,512]{2,1,0:T(8,128)(2,1)S(1)}, u32[]{:S(2)}, u32[]{:S(2)}) collective-permute-start(bf16[2,80,512]{2,1,0:T(8,128)(2,1)S(1)} %get-tuple-element.27), channel_id=1, source_target_pairs={{0,24},{4,28},{8,16},{12,20},{16,8},{20,12},{24,0},{28,4},{1,25},{... | collective-permute-start | bytes 491528 | tf_op jit(solution)/shard_map/ppermute | solution.py:16
  102.5 7.4 %collective-permute-start.23 = (bf16[80,512]{1,0:T(8,128)(2,1)S(1)}, bf16[80,512]{1,0:T(8,128)(2,1)S(1)}, u32[]{:S(2)}, u32[]{:S(2)}) collective-permute-start(bf16[80,512]{1,0:T(8,128)(2,1)S(1)} %fusion.14), channel_id=1, source_target_pairs={{0,4},{4,0},{8,12},{12,8},{16,20},{20,16},{24,28},{28,24},{1,5},{5... | collective-permute-start | bytes 245768 | tf_op jit(solution)/shard_map/ppermute | solution.py:16
  109.9 5.2 %copy-start.2 = (bf16[2048,512]{1,0:T(8,128)(2,1)S(1)}, bf16[2048,512]{1,0:T(8,128)(2,1)}, u32[]{:S(2)}) copy-start(bf16[2048,512]{1,0:T(8,128)(2,1)} %refs_7_.3) | copy-start | bytes 6291460
  109.9 11.0 %collective-permute-start.4 = (bf16[512,512]{1,0:T(8,128)(2,1)S(1)}, bf16[512,512]{1,0:T(8,128)(2,1)S(1)}, u32[]{:S(2)}, u32[]{:S(2)}) collective-permute-start(bf16[512,512]{1,0:T(8,128)(2,1)S(1)} %bitcast.82), channel_id=1, source_target_pairs={{0,1},{1,0},{2,3},{3,2},{4,5},{5,4},{6,7},{7,6},{8,9},{9,8},{10,11... | collective-permute-start | bytes 1572872 | tf_op jit(solution)/shard_map/ppermute | solution.py:16
  109.9 11.0 %collective-permute-start.6 = (bf16[512,512]{1,0:T(8,128)(2,1)S(1)}, bf16[512,512]{1,0:T(8,128)(2,1)S(1)}, u32[]{:S(2)}, u32[]{:S(2)}) collective-permute-start(bf16[512,512]{1,0:T(8,128)(2,1)S(1)} %collective-permute-done.5.refs_2_), channel_id=1, source_target_pairs={{0,1},{1,0},{2,3},{3,2},{4,5},{5,4},{6,7},{7,6},{8,9},{9,8},{10,11... | collective-permute-start | bytes 1572872 | tf_op jit(solution)/shard_map/ppermute | solution.py:16
  110.6 14.1 %collective-permute-start.17 = (bf16[176,512]{1,0:T(8,128)(2,1)S(1)}, bf16[176,512]{1,0:T(8,128)(2,1)S(1)}, u32[]{:S(2)}, u32[]{:S(2)}) collective-permute-start(bf16[176,512]{1,0:T(8,128)(2,1)S(1)} %get-tuple-element.30), channel_id=1, source_target_pairs={{0,8},{4,12},{8,0},{12,4},{16,24},{20,28},{24,16},{28,20},{1,9},{5... | collective-permute-start | bytes 540680 | tf_op jit(solution)/shard_map/ppermute | solution.py:16
  110.7 16.2 %collective-permute-start.18 = (bf16[176,512]{1,0:T(8,128)(2,1)S(1)}, bf16[176,512]{1,0:T(8,128)(2,1)S(1)}, u32[]{:S(2)}, u32[]{:S(2)}) collective-permute-start(bf16[176,512]{1,0:T(8,128)(2,1)S(1)} %get-tuple-element.32), channel_id=1, source_target_pairs={{0,16},{4,20},{8,24},{12,28},{16,0},{20,4},{24,8},{28,12},{1,17},{... | collective-permute-start | bytes 540680 | tf_op jit(solution)/shard_map/ppermute | solution.py:16
  111.3 15.6 %collective-permute-start.19 = (bf16[176,512]{1,0:T(8,128)(2,1)S(1)}, bf16[176,512]{1,0:T(8,128)(2,1)S(1)}, u32[]{:S(2)}, u32[]{:S(2)}) collective-permute-start(bf16[176,512]{1,0:T(8,128)(2,1)S(1)} %get-tuple-element.31), channel_id=1, source_target_pairs={{0,24},{4,28},{8,16},{12,20},{16,8},{20,12},{24,0},{28,4},{1,25},{... | collective-permute-start | bytes 540680 | tf_op jit(solution)/shard_map/ppermute | solution.py:16

commit v3 on v2

--- a/solution.py
+++ b/solution.py
@@ -193,38 +193,71 @@
     return [pieces[d] for d in range(count)]
 
 
-def prior_kernel(pieces, ids_ref, *refs):
-    tree_ref, out_ref = refs[2 * pieces], refs[2 * pieces + 1]
-    total = None
-    for at in range(pieces):
-        part = jnp.dot(refs[at][...], refs[pieces + at][...], preferred_element_type=jnp.float32)
-        total = part if total is None else total + part
-    out_ref[...] = tree_ref[...] - total
-
-
-def minus_prior(tree, pieces, precision, ids, row_of, block):
+def prior_kernel(count, chunks, ids_ref, *refs):
+    pieces, precision_ref, tree_ref = refs[:count], refs[count], refs[count + 1]
+    out_ref, held, in_sem, out_sem = refs[count + 2 :]
+    columns = precision_ref.shape[1]
+    width = columns // 2
+    depth = pieces[0].shape[1]
+
+    def copies(at, outward):
+        made, row = [], 0
+        for part, (first, length) in enumerate(chunks[at]):
+            here = held.at[at, pl.ds(row, length)]
+            there = pl.ds(first, length)
+            if outward:
+                made.append(pltpu.make_async_copy(here, out_ref.at[there], out_sem.at[at, part]))
+            else:
+                made.append(pltpu.make_async_copy(tree_ref.at[there], here, in_sem.at[at, part]))
+            row += length
+        return made
+
+    for at in range(len(chunks)):
+        for copy in copies(at, False):
+            copy.start()
+    rows = held.shape[1]
+    for at in range(len(chunks)):
+        left = jnp.concatenate([piece[at * rows : (at + 1) * rows, :] for piece in pieces], axis=1)
+        for half in range(2):
+            cols = slice(half * width, (half + 1) * width)
+            firsts = [pl.multiple_of((ids_ref[0] ^ d) * depth, depth) for d in range(count)]
+            weight = jnp.concatenate([precision_ref[pl.ds(first, depth), cols] for first in firsts], axis=0)
+            total = jnp.dot(left, weight, preferred_element_type=jnp.float32)
+            if half == 0:
+                for copy in copies(at, False):
+                    copy.wait()
+            held[at, :, cols] -= total
+        for copy in copies(at, True):
+            copy.start()
+    for at in range(len(chunks)):
+        for copy in copies(at, True):
+            copy.wait()
+
+
+def minus_prior(tree, pieces, precision, ids, chunks):
     plots, columns = pieces[0].shape
     count = len(pieces)
-    held = pl.BlockSpec((block, columns), lambda i, ids: (row_of(i), 0))
-    weight = lambda d: pl.BlockSpec((columns, columns), lambda i, ids: (ids[0] ^ d, 0))
+    rows = plots // len(chunks)
+    parts = len(chunks[0])
+    vmem = pl.BlockSpec(memory_space=pltpu.VMEM)
+    hbm = pl.BlockSpec(memory_space=pltpu.HBM)
     return pl.pallas_call(
-        functools.partial(prior_kernel, count),
-        grid_spec=pltpu.PrefetchScalarGridSpec(
-            num_scalar_prefetch=1,
-            grid=(plots // block,),
-            in_specs=[pl.BlockSpec((block, columns), lambda i, ids: (i, 0))] * count
-            + [weight(d) for d in range(count)]
-            + [held],
-            out_specs=held,
-        ),
+        functools.partial(prior_kernel, count, chunks),
+        in_specs=[pl.BlockSpec(memory_space=pltpu.SMEM)] + [vmem] * (count + 1) + [hbm],
+        out_specs=hbm,
         out_shape=jax.ShapeDtypeStruct(tree.shape, tree.dtype),
-        input_output_aliases={2 * count + 1: 0},
+        input_output_aliases={count + 2: 0},
+        scratch_shapes=[
+            pltpu.VMEM((len(chunks), rows, columns), jnp.float32),
+            pltpu.SemaphoreType.DMA((len(chunks), parts)),
+            pltpu.SemaphoreType.DMA((len(chunks), parts)),
+        ],
         cost_estimate=pl.CostEstimate(
             flops=2 * count * plots * columns * columns, bytes_accessed=16 * plots * columns, transcendentals=0
         ),
         compiler_params=pltpu.CompilerParams(vmem_limit_bytes=16 << 20),
         name="prior",
-    )(ids, *pieces, *([precision] * count), tree)
+    )(ids, *pieces, precision, tree)
 
 
 def pick_kernel(split, ids_ref, blocks_ref, *outs):
@@ -327,8 +360,12 @@
         above_k, (top_wide, 0), (mid_wide, 0), (mid_wide, rows - 3), (bottom_wide, 0), below_k, kappa, False
     )
     spatial_edge_pieces = gather_pieces(flat(spatial_edge))
-    grad = minus_prior(tree, spatial_mid_pieces, species_precision, ids, lambda i: i + 1, cols)
-    grad = minus_prior(grad, spatial_edge_pieces, species_precision, ids, lambda i: i * (rows - 1), cols)
+    middle = (rows - 2) * cols
+    half = middle // 2
+    chunks = (((cols, half),), ((cols + half, half),))
+    grad = minus_prior(tree, spatial_mid_pieces, species_precision, ids, chunks)
+    chunks = (((0, cols), (plots - cols, cols)),)
+    grad = minus_prior(grad, spatial_edge_pieces, species_precision, ids, chunks)
     return (grad.reshape(rows, cols, columns), gram)
 
 

time: 129 us -> 129 us (level)
  no operation moved by 1% of the time
where the time goes in v3:
time: 129 us; the launch traced here: 128 us
  Pallas kernels  40.2 us (31%)
  starting transfers between devices  40.1 us (31%)
  waiting for transfers between devices  37 us (29%)
  matrix products  4.79 us (4%)
  local copies, waits for them, and re-layouts  3.18 us (2%)
  other arithmetic  1.54 us (1%)
    ppermute x20, starting transfers between devices, xor_swap(): return lax.ppermute(value, axis, [(i, i ^ mask) for i in range(count)])  28.1 us
    ppermute x20, waiting for transfers between devices, xor_swap(): return lax.ppermute(value, axis, [(i, i ^ mask) for i in range(count)])  21.9 us
    pallas_call x3, Pallas kernels, tree_term(): pl.pallas_call(functools.partial(tree_kernel, columns // LANES, first), g...  20.5 us
    ppermute x2, waiting for transfers between devices, halo(): above = lax.ppermute(last, 'space', forward)  15.2 us
    pallas_call x2, Pallas kernels, minus_prior(): pl.pallas_call(functools.partial(prior_kernel, count, chunks), in_specs=[...  10.7 us
    ppermute x2, starting transfers between devices, halo(): above = lax.ppermute(last, 'space', forward)  9.34 us
    dot_general x8, matrix products, product(): lax.dot_general(left, right, (((0,), (0,)), ((), ())), preferred_element_...  4.79 us
    pallas_call x2, Pallas kernels, stencil_mid(): pl.pallas_call(functools.partial(mid_kernel, rows, with_wide), grid=(colu...  4.68 us
  transfers between devices with their start and end apart: 24, of which 4 were waited for; matrix products, arithmetic and copies ran while one was open for 4% of the time, Pallas kernels for 31%

profile of v3, /device:TPU:0, one launch (start us, length us, event | category | flops | bytes accessed | tf_op | source)
XLA Modules:
  0.0 127.8 jit_solution(6879644230856057647)
XLA Ops:
  0.6 0.1 pad_add_fusion.first_ref.ids_ref
  0.7 1.3 fusion.15
  2.0 4.9 %collective-permute-start = (f32[1,256,512]{2,1,0:T(8,128)S(1)}, f32[1,256,512]{2,1,0:T(8,128)S(1)}, u32[]{:S(2)}, u32[]{:S(2)}) collective-permute-start(f32[1,256,512]{2,1,0:T(8,128)S(1)} %get-tuple-element.29), channel_id=1, source_target_pairs={{0,4},{4,8},{8,12},{12,16},{16,20},{20,24},{24,28},{1,5},{5,9},{9,... | collective-permute-start | bytes 1572872 | tf_op jit(solution)/shard_map/ppermute | solution.py:181
  6.9 1.3 %collective-permute-start.1 = (f32[1,256,512]{2,1,0:T(8,128)S(1)}, f32[1,256,512]{2,1,0:T(8,128)S(1)}, u32[]{:S(2)}, u32[]{:S(2)}) collective-permute-start(f32[1,256,512]{2,1,0:T(8,128)S(1)} %get-tuple-element.28), channel_id=1, source_target_pairs={{4,0},{8,4},{12,8},{16,12},{20,16},{24,20},{28,24},{5,1},{9,5},{13... | collective-permute-start | bytes 1572872 | tf_op jit(solution)/shard_map/ppermute | solution.py:182
  8.3 1.9 %copy-done = f32[6,256,512]{2,1,0:T(8,128)S(1)} copy-done((f32[6,256,512]{2,1,0:T(8,128)S(1)}, f32[6,256,512]{2,1,0:T(8,128)}, u32[]{:S(2)}) %copy-start) | copy-done | bytes 3145752
  10.1 2.4 %stencil_mid.2 = (bf16[4,256,512]{2,1,0:T(8,128)(2,1)S(1)}, f32[4,256,512]{2,1,0:T(8,128)S(1)}) custom-call(f32[6,256,512]{2,1,0:T(8,128)S(1)} %copy-done, f32[6,256]{1,0:T(8,128)S(1)} %copy-done.5), custom_call_target="tpu_custom_call" | custom-call | flops 6291456 | bytes 7864320 | tf_op jit(solution)/shard_map/stencil_mid/pallas_call | solution.py:146
  12.6 1.6 %collective-permute-start.12 = (bf16[1024,512]{1,0:T(8,128)(2,1)S(1)}, bf16[1024,512]{1,0:T(8,128)(2,1)S(1)}, u32[]{:S(2)}, u32[]{:S(2)}) collective-permute-start(bf16[1024,512]{1,0:T(8,128)(2,1)S(1)} %bitcast.87), channel_id=1, source_target_pairs={{0,2},{1,3},{2,0},{3,1},{4,6},{5,7},{6,4},{7,5},{8,10},{9,11},{10,... | collective-permute-start | bytes 3145736 | tf_op jit(solution)/shard_map/ppermute | solution.py:16
  14.2 15.2 %collective-permute-done.above_ref = f32[1,256,512]{2,1,0:T(8,128)S(1)} collective-permute-done((f32[1,256,512]{2,1,0:T(8,128)S(1)}, f32[1,256,512]{2,1,0:T(8,128)S(1)}, u32[]{:S(2)}, u32[]{:S(2)}) %collective-permute-start) | collective-permute-done | bytes 524320 | tf_op jit(solution)/shard_map/ppermute | solution.py:181
  29.3 1.9 %stencil_edge.2 = (bf16[2,256,512]{2,1,0:T(8,128)(2,1)S(1)}, f32[1,256,512]{2,1,0:T(8,128)S(1)}, f32[1,256,512]{2,1,0:T(8,128)S(1)}) custom-call(f32[1,256,512]{2,1,0:T(8,128)S(1)} %collective-permute-done.above_ref, f32[6,256,512]{2,1,0:T(8,128)S(1)} %copy-done.1, f32[6,256,512]{2,1,0:T(8,128)S(1)} %copy-done.1, f32[6,256,512]{2,1,0:T(8,128)S(1)} %copy-done.1, ...), custom_call_target="tpu_custom_call" | custom-call | flops 2097152 | bytes 4718592 | tf_op jit(solution)/shard_map/stencil_edge/pallas_call | solution.py:165
  31.2 1.6 %collective-permute-start.13 = (bf16[512,512]{1,0:T(8,128)(2,1)S(1)}, bf16[512,512]{1,0:T(8,128)(2,1)S(1)}, u32[]{:S(2)}, u32[]{:S(2)}) collective-permute-start(bf16[512,512]{1,0:T(8,128)(2,1)S(1)} %bitcast.66), channel_id=1, source_target_pairs={{0,2},{1,3},{2,0},{3,1},{4,6},{5,7},{6,4},{7,5},{8,10},{9,11},{10,... | collective-permute-start | bytes 1572872 | tf_op jit(solution)/shard_map/ppermute | solution.py:16
  32.8 0.7 convolution_bitcast_fusion.1
  33.5 0.6 collective-permute-start.11
  34.1 4.4 %collective-permute-start.2 = (f32[1,256,512]{2,1,0:T(8,128)S(1)}, f32[1,256,512]{2,1,0:T(8,128)S(1)}, u32[]{:S(2)}, u32[]{:S(2)}) collective-permute-start(f32[1,256,512]{2,1,0:T(8,128)S(1)} %get-tuple-element.17.last_ref.refs_2_), channel_id=1, source_target_pairs={{0,4},{4,8},{8,12},{12,16},{16,20},{20,24},{24,28},{1,5},{5,9},{9,... | collective-permute-start | bytes 1572872 | tf_op jit(solution)/shard_map/ppermute | solution.py:181
  38.5 2.2 %stencil_mid.3 = bf16[4,256,512]{2,1,0:T(8,128)(2,1)S(1)} custom-call(f32[4,256,512]{2,1,0:T(8,128)S(1)} %get-tuple-element.19.second_ref.before_ref.refs_0_, f32[1,256,512]{2,1,0:T(8,128)S(1)} %get-tuple-element.18.first_ref.refs_1_, f32[1,256,512]{2,1,0:T(8,128)S(1)} %get-tuple-element.17.last_ref.refs_2_, f32[6,256]{1,0:T(8,128)S(1)} %copy-done.5), custom_call_target="tpu_custom_call" | custom-call | flops 4194304 | bytes 5242880 | tf_op jit(solution)/shard_map/stencil_mid/pallas_call | solution.py:146
  40.7 0.5 fusion.5
  41.2 7.3 %collective-permute-done.13 = bf16[512,512]{1,0:T(8,128)(2,1)S(1)} collective-permute-done((bf16[512,512]{1,0:T(8,128)(2,1)S(1)}, bf16[512,512]{1,0:T(8,128)(2,1)S(1)}, u32[]{:S(2)}, u32[]{:S(2)}) %collective-permute-start.13) | collective-permute-done | bytes 524320 | tf_op jit(solution)/shard_map/ppermute | solution.py:16
  48.5 1.5 %collective-permute-start.3 = (f32[1,256,512]{2,1,0:T(8,128)S(1)}, f32[1,256,512]{2,1,0:T(8,128)S(1)}, u32[]{:S(2)}, u32[]{:S(2)}) collective-permute-start(f32[1,256,512]{2,1,0:T(8,128)S(1)} %get-tuple-element.18.first_ref.refs_1_), channel_id=1, source_target_pairs={{4,0},{8,4},{12,8},{16,12},{20,16},{24,20},{28,24},{5,1},{9,5},{13... | collective-permute-start | bytes 1572872 | tf_op jit(solution)/shard_map/ppermute | solution.py:182
  50.0 0.1 collective-permute-start.14
  50.1 0.5 fusion.17
  50.5 0.7 fusion.7
  51.3 0.6 collective-permute-start.15
  51.8 0.5 fusion.16
  52.3 1.6 %collective-permute-start.8 = (bf16[1024,512]{1,0:T(8,128)(2,1)S(1)}, bf16[1024,512]{1,0:T(8,128)(2,1)S(1)}, u32[]{:S(2)}, u32[]{:S(2)}) collective-permute-start(bf16[1024,512]{1,0:T(8,128)(2,1)S(1)} %bitcast.78), channel_id=1, source_target_pairs={{0,2},{1,3},{2,0},{3,1},{4,6},{5,7},{6,4},{7,5},{8,10},{9,11},{10,... | collective-permute-start | bytes 3145736 | tf_op jit(solution)/shard_map/ppermute | solution.py:16
  53.9 0.7 fusion.8
  54.6 0.5 fusion.18
  55.1 0.7 fusion.6
  55.8 0.3 pad_maximum_fusion
  56.1 0.7 pick.1
  56.8 4.5 %collective-permute-start.20 = (bf16[2,80,512]{2,1,0:T(8,128)(2,1)S(1)}, bf16[2,80,512]{2,1,0:T(8,128)(2,1)S(1)}, u32[]{:S(2)}, u32[]{:S(2)}) collective-permute-start(bf16[2,80,512]{2,1,0:T(8,128)(2,1)S(1)} %get-tuple-element.25), channel_id=1, source_target_pairs={{0,8},{4,12},{8,0},{12,4},{16,24},{20,28},{24,16},{28,20},{1,9},{5... | collective-permute-start | bytes 491528 | tf_op jit(solution)/shard_map/ppermute | solution.py:16
  61.3 2.6 %collective-permute-start.21 = (bf16[2,80,512]{2,1,0:T(8,128)(2,1)S(1)}, bf16[2,80,512]{2,1,0:T(8,128)(2,1)S(1)}, u32[]{:S(2)}, u32[]{:S(2)}) collective-permute-start(bf16[2,80,512]{2,1,0:T(8,128)(2,1)S(1)} %get-tuple-element.26), channel_id=1, source_target_pairs={{0,16},{4,20},{8,24},{12,28},{16,0},{20,4},{24,8},{28,12},{1,17},{... | collective-permute-start | bytes 491528 | tf_op jit(solution)/shard_map/ppermute | solution.py:16
  64.0 13.5 %collective-permute-done.8.refs_2_ = bf16[1024,512]{1,0:T(8,128)(2,1)S(1)} collective-permute-done((bf16[1024,512]{1,0:T(8,128)(2,1)S(1)}, bf16[1024,512]{1,0:T(8,128)(2,1)S(1)}, u32[]{:S(2)}, u32[]{:S(2)}) %collective-permute-start.8) | collective-permute-done | bytes 1048608 | tf_op jit(solution)/shard_map/ppermute | solution.py:16
  77.5 1.8 %stencil_edge.3 = bf16[2,256,512]{2,1,0:T(8,128)(2,1)S(1)} custom-call(f32[1,256,512]{2,1,0:T(8,128)S(1)} %collective-permute-done.2.above_ref, f32[1,256,512]{2,1,0:T(8,128)S(1)} %get-tuple-element.18.first_ref.refs_1_, f32[4,256,512]{2,1,0:T(8,128)S(1)} %get-tuple-element.19.second_ref.before_ref.refs_0_, ...), custom_call_target="tpu_custom_call" | custom-call | flops 2097152 | bytes 4718592 | tf_op jit(solution)/shard_map/stencil_edge/pallas_call | solution.py:165
  79.3 1.6 %collective-permute-start.5 = (bf16[512,512]{1,0:T(8,128)(2,1)S(1)}, bf16[512,512]{1,0:T(8,128)(2,1)S(1)}, u32[]{:S(2)}, u32[]{:S(2)}) collective-permute-start(bf16[512,512]{1,0:T(8,128)(2,1)S(1)} %bitcast.81), channel_id=1, source_target_pairs={{0,2},{1,3},{2,0},{3,1},{4,6},{5,7},{6,4},{7,5},{8,10},{9,11},{10,... | collective-permute-start | bytes 1572872 | tf_op jit(solution)/shard_map/ppermute | solution.py:16
  80.8 3.0 %collective-permute-start.16 = (bf16[4,176,512]{2,1,0:T(8,128)(2,1)S(1)}, bf16[4,176,512]{2,1,0:T(8,128)(2,1)S(1)}, u32[]{:S(2)}, u32[]{:S(2)}) collective-permute-start(bf16[4,176,512]{2,1,0:T(8,128)(2,1)S(1)} %get-tuple-element.23), channel_id=1, source_target_pairs={{0,4},{4,0},{8,12},{12,8},{16,20},{20,16},{24,28},{28,24},{1,5},{5... | collective-permute-start | bytes 2162696 | tf_op jit(solution)/shard_map/ppermute | solution.py:16
  83.8 5.0 %collective-permute-start.22 = (bf16[2,80,512]{2,1,0:T(8,128)(2,1)S(1)}, bf16[2,80,512]{2,1,0:T(8,128)(2,1)S(1)}, u32[]{:S(2)}, u32[]{:S(2)}) collective-permute-start(bf16[2,80,512]{2,1,0:T(8,128)(2,1)S(1)} %get-tuple-element.27), channel_id=1, source_target_pairs={{0,24},{4,28},{8,16},{12,20},{16,8},{20,12},{24,0},{28,4},{1,25},{... | collective-permute-start | bytes 491528 | tf_op jit(solution)/shard_map/ppermute | solution.py:16
  88.8 6.8 %tree_term.3.rest_0_ = f32[1536,512]{1,0:T(8,128)} custom-call(s32[4]{0:T(128)S(1)} %pad_add_fusion.first_ref.ids_ref, f32[1536,512]{1,0:T(8,128)S(1)} %bitcast.63, f32[1536,128]{1,0:T(8,128)S(1)} %bitcast.72, s32[1536,128]{1,0:T(8,128)S(1)} %bitcast.75, s32[6,256]{1,0:T(8,128)S(1)} %copy-done.6, f32[1,512]{1,0:T(1,128)S(1)} %bitcast.84), custom_call_target="tpu_custom_call" | custom-call | flops 1073741824 | bytes 2621440 | tf_op jit(solution)/shard_map/tree_term/pallas_call | solution.py:77
  95.7 6.8 %tree_term.4.rest_0_ = f32[1536,512]{1,0:T(8,128)} custom-call(s32[4]{0:T(128)S(1)} %pad_add_fusion.first_ref.ids_ref, f32[1536,512]{1,0:T(8,128)S(1)} %bitcast.64, f32[1536,128]{1,0:T(8,128)S(1)} %bitcast.73, s32[1536,128]{1,0:T(8,128)S(1)} %bitcast.76, s32[6,256]{1,0:T(8,128)S(1)} %copy-done.6, ...), custom_call_target="tpu_custom_call", output_to_operand_aliasing={{}: (6, {})} | custom-call | flops 1073741824 | bytes 2621440 | tf_op jit(solution)/shard_map/tree_term/pallas_call | solution.py:77
  102.5 0.6 collective-permute-start.23
  103.1 6.8 %tree_term.5.refs_5_ = f32[1536,512]{1,0:T(8,128)} custom-call(s32[4]{0:T(128)S(1)} %pad_add_fusion.first_ref.ids_ref, f32[1536,512]{1,0:T(8,128)S(1)} %bitcast.65, f32[1536,128]{1,0:T(8,128)S(1)} %bitcast.74, s32[1536,128]{1,0:T(8,128)S(1)} %bitcast.77, s32[6,256]{1,0:T(8,128)S(1)} %copy-done.6, ...), custom_call_target="tpu_custom_call", output_to_operand_aliasing={{}: (6, {})} | custom-call | flops 1073741824 | bytes 2621440 | tf_op jit(solution)/shard_map/tree_term/pallas_call | solution.py:77
  109.9 0.5 collective-permute-start.6
  110.5 0.1 fusion.11
  110.7 0.6 collective-permute-start.18
  111.3 3.8 %collective-permute-start.19 = (bf16[176,512]{1,0:T(8,128)(2,1)S(1)}, bf16[176,512]{1,0:T(8,128)(2,1)S(1)}, u32[]{:S(2)}, u32[]{:S(2)}) collective-permute-start(bf16[176,512]{1,0:T(8,128)(2,1)S(1)} %get-tuple-element.31), channel_id=1, source_target_pairs={{0,24},{4,28},{8,16},{12,20},{16,8},{20,12},{24,0},{28,4},{1,25},{... | collective-permute-start | bytes 540680 | tf_op jit(solution)/shard_map/ppermute | solution.py:16
  115.1 5.6 %prior.2.refs_5_ = f32[1536,512]{1,0:T(8,128)} custom-call(s32[4]{0:T(128)S(1)} %pad_add_fusion.first_ref.ids_ref, bf16[1024,512]{1,0:T(8,128)(2,1)S(1)} %bitcast.80, bf16[1024,512]{1,0:T(8,128)(2,1)S(1)} %collective-permute-done.7.refs_1_, bf16[1024,512]{1,0:T(8,128)(2,1)S(1)} %collective-permute-done.8.refs_2_, ...), custom_call_target="tpu_custom_call", output_to_operand_aliasing={{}: (6, {})} | custom-call | flops 2147483648 | bytes 8388608 | tf_op jit(solution)/shard_map/prior/pallas_call | solution.py:244
  120.7 5.1 %prior.3 = f32[1536,512]{1,0:T(8,128)} custom-call(s32[4]{0:T(128)S(1)} %pad_add_fusion.first_ref.ids_ref, bf16[512,512]{1,0:T(8,128)(2,1)S(1)} %bitcast.83, bf16[512,512]{1,0:T(8,128)(2,1)S(1)} %collective-permute-done.4.refs_1_, bf16[512,512]{1,0:T(8,128)(2,1)S(1)} %collective-permute-done.5.refs_2_, ...), custom_call_target="tpu_custom_call", output_to_operand_aliasing={{}: (6, {})} | custom-call | flops 1073741824 | bytes 4194304 | tf_op jit(solution)/shard_map/prior/pallas_call | solution.py:244
  125.8 1.0 collective-permute-done.18
  126.9 0.1 fusion.10
  127.0 0.9 maximum_multiply_fusion
  (42 shorter events, 0.3 us)
Async XLA Ops:
  0.6 7.6 %copy-start.5 = (f32[6,256]{1,0:T(8,128)S(1)}, f32[6,256]{1,0:T(8,128)}, u32[]{:S(2)}) copy-start(f32[6,256]{1,0:T(8,128)} %refs_3_.1) | copy-start | bytes 18436
  2.0 27.3 %collective-permute-start = (f32[1,256,512]{2,1,0:T(8,128)S(1)}, f32[1,256,512]{2,1,0:T(8,128)S(1)}, u32[]{:S(2)}, u32[]{:S(2)}) collective-permute-start(f32[1,256,512]{2,1,0:T(8,128)S(1)} %get-tuple-element.29), channel_id=1, source_target_pairs={{0,4},{4,8},{8,12},{12,16},{16,20},{20,24},{24,28},{1,5},{5,9},{9,... | collective-permute-start | bytes 1572872 | tf_op jit(solution)/shard_map/ppermute | solution.py:181
  6.9 22.4 %collective-permute-start.1 = (f32[1,256,512]{2,1,0:T(8,128)S(1)}, f32[1,256,512]{2,1,0:T(8,128)S(1)}, u32[]{:S(2)}, u32[]{:S(2)}) collective-permute-start(f32[1,256,512]{2,1,0:T(8,128)S(1)} %get-tuple-element.28), channel_id=1, source_target_pairs={{4,0},{8,4},{12,8},{16,12},{20,16},{24,20},{28,24},{5,1},{9,5},{13... | collective-permute-start | bytes 1572872 | tf_op jit(solution)/shard_map/ppermute | solution.py:182
  8.2 1.9 %copy-start = (f32[6,256,512]{2,1,0:T(8,128)S(1)}, f32[6,256,512]{2,1,0:T(8,128)}, u32[]{:S(2)}) copy-start(f32[6,256,512]{2,1,0:T(8,128)} %refs_0_) | copy-start | bytes 9437188
  10.1 19.2 %copy-start.1 = (f32[6,256,512]{2,1,0:T(8,128)S(1)}, f32[6,256,512]{2,1,0:T(8,128)}, u32[]{:S(2)}) copy-start(f32[6,256,512]{2,1,0:T(8,128)} %refs_0_) | copy-start | bytes 9437188
  12.6 37.4 %collective-permute-start.12 = (bf16[1024,512]{1,0:T(8,128)(2,1)S(1)}, bf16[1024,512]{1,0:T(8,128)(2,1)S(1)}, u32[]{:S(2)}, u32[]{:S(2)}) collective-permute-start(bf16[1024,512]{1,0:T(8,128)(2,1)S(1)} %bitcast.87), channel_id=1, source_target_pairs={{0,2},{1,3},{2,0},{3,1},{4,6},{5,7},{6,4},{7,5},{8,10},{9,11},{10,... | collective-permute-start | bytes 3145736 | tf_op jit(solution)/shard_map/ppermute | solution.py:16
  31.2 17.3 %collective-permute-start.13 = (bf16[512,512]{1,0:T(8,128)(2,1)S(1)}, bf16[512,512]{1,0:T(8,128)(2,1)S(1)}, u32[]{:S(2)}, u32[]{:S(2)}) collective-permute-start(bf16[512,512]{1,0:T(8,128)(2,1)S(1)} %bitcast.66), channel_id=1, source_target_pairs={{0,2},{1,3},{2,0},{3,1},{4,6},{5,7},{6,4},{7,5},{8,10},{9,11},{10,... | collective-permute-start | bytes 1572872 | tf_op jit(solution)/shard_map/ppermute | solution.py:16
  32.8 19.5 %collective-permute-start.10 = (bf16[1024,512]{1,0:T(8,128)(2,1)S(1)}, bf16[1024,512]{1,0:T(8,128)(2,1)S(1)}, u32[]{:S(2)}, u32[]{:S(2)}) collective-permute-start(bf16[1024,512]{1,0:T(8,128)(2,1)S(1)} %bitcast.88), channel_id=1, source_target_pairs={{0,1},{1,0},{2,3},{3,2},{4,5},{5,4},{6,7},{7,6},{8,9},{9,8},{10,11... | collective-permute-start | bytes 3145736 | tf_op jit(solution)/shard_map/ppermute | solution.py:16
  33.5 17.8 %collective-permute-start.11 = (bf16[512,512]{1,0:T(8,128)(2,1)S(1)}, bf16[512,512]{1,0:T(8,128)(2,1)S(1)}, u32[]{:S(2)}, u32[]{:S(2)}) collective-permute-start(bf16[512,512]{1,0:T(8,128)(2,1)S(1)} %bitcast.67), channel_id=1, source_target_pairs={{0,1},{1,0},{2,3},{3,2},{4,5},{5,4},{6,7},{7,6},{8,9},{9,8},{10,11... | collective-permute-start | bytes 1572872 | tf_op jit(solution)/shard_map/ppermute | solution.py:16
  34.1 29.9 %collective-permute-start.2 = (f32[1,256,512]{2,1,0:T(8,128)S(1)}, f32[1,256,512]{2,1,0:T(8,128)S(1)}, u32[]{:S(2)}, u32[]{:S(2)}) collective-permute-start(f32[1,256,512]{2,1,0:T(8,128)S(1)} %get-tuple-element.17.last_ref.refs_2_), channel_id=1, source_target_pairs={{0,4},{4,8},{8,12},{12,16},{16,20},{20,24},{24,28},{1,5},{5,9},{9,... | collective-permute-start | bytes 1572872 | tf_op jit(solution)/shard_map/ppermute | solution.py:181
  48.5 29.0 %collective-permute-start.3 = (f32[1,256,512]{2,1,0:T(8,128)S(1)}, f32[1,256,512]{2,1,0:T(8,128)S(1)}, u32[]{:S(2)}, u32[]{:S(2)}) collective-permute-start(f32[1,256,512]{2,1,0:T(8,128)S(1)} %get-tuple-element.18.first_ref.refs_1_), channel_id=1, source_target_pairs={{4,0},{8,4},{12,8},{16,12},{20,16},{24,20},{28,24},{5,1},{9,5},{13... | collective-permute-start | bytes 1572872 | tf_op jit(solution)/shard_map/ppermute | solution.py:182
  50.0 5.1 %collective-permute-start.14 = (bf16[1024,512]{1,0:T(8,128)(2,1)S(1)}, bf16[1024,512]{1,0:T(8,128)(2,1)S(1)}, u32[]{:S(2)}, u32[]{:S(2)}) collective-permute-start(bf16[1024,512]{1,0:T(8,128)(2,1)S(1)} %collective-permute-done.12), channel_id=1, source_target_pairs={{0,1},{1,0},{2,3},{3,2},{4,5},{5,4},{6,7},{7,6},{8,9},{9,8},{10,11... | collective-permute-start | bytes 3145736 | tf_op jit(solution)/shard_map/ppermute | solution.py:16
  51.3 3.3 %collective-permute-start.15 = (bf16[512,512]{1,0:T(8,128)(2,1)S(1)}, bf16[512,512]{1,0:T(8,128)(2,1)S(1)}, u32[]{:S(2)}, u32[]{:S(2)}) collective-permute-start(bf16[512,512]{1,0:T(8,128)(2,1)S(1)} %collective-permute-done.13), channel_id=1, source_target_pairs={{0,1},{1,0},{2,3},{3,2},{4,5},{5,4},{6,7},{7,6},{8,9},{9,8},{10,11... | collective-permute-start | bytes 1572872 | tf_op jit(solution)/shard_map/ppermute | solution.py:16
  52.3 25.1 %collective-permute-start.8 = (bf16[1024,512]{1,0:T(8,128)(2,1)S(1)}, bf16[1024,512]{1,0:T(8,128)(2,1)S(1)}, u32[]{:S(2)}, u32[]{:S(2)}) collective-permute-start(bf16[1024,512]{1,0:T(8,128)(2,1)S(1)} %bitcast.78), channel_id=1, source_target_pairs={{0,2},{1,3},{2,0},{3,1},{4,6},{5,7},{6,4},{7,5},{8,10},{9,11},{10,... | collective-permute-start | bytes 3145736 | tf_op jit(solution)/shard_map/ppermute | solution.py:16
  56.8 24.0 %collective-permute-start.20 = (bf16[2,80,512]{2,1,0:T(8,128)(2,1)S(1)}, bf16[2,80,512]{2,1,0:T(8,128)(2,1)S(1)}, u32[]{:S(2)}, u32[]{:S(2)}) collective-permute-start(bf16[2,80,512]{2,1,0:T(8,128)(2,1)S(1)} %get-tuple-element.25), channel_id=1, source_target_pairs={{0,8},{4,12},{8,0},{12,4},{16,24},{20,28},{24,16},{28,20},{1,9},{5... | collective-permute-start | bytes 491528 | tf_op jit(solution)/shard_map/ppermute | solution.py:16
  61.3 27.5 %copy-start.3 = (f32[6,256,128]{2,1,0:T(8,128)S(1)}, f32[6,256,128]{2,1,0:T(8,128)}, u32[]{:S(2)}) copy-start(f32[6,256,128]{2,1,0:T(8,128)} %param.9) | copy-start | bytes 2359300
  61.3 27.5 %copy-start.4 = (s32[6,256,128]{2,1,0:T(8,128)S(1)}, s32[6,256,128]{2,1,0:T(8,128)}, u32[]{:S(2)}) copy-start(s32[6,256,128]{2,1,0:T(8,128)} %param.10) | copy-start | bytes 2359300
  61.3 27.5 %copy-start.6 = (s32[6,256]{1,0:T(8,128)S(1)}, s32[6,256]{1,0:T(8,128)}, u32[]{:S(2)}) copy-start(s32[6,256]{1,0:T(8,128)} %counts_ref.5) | copy-start | bytes 18436
  61.3 27.5 %copy-start.7 = (f32[512]{0:T(512)S(1)}, f32[512]{0:T(512)}, u32[]{:S(2)}) copy-start(f32[512]{0:T(512)} %param.12) | copy-start | bytes 6148
  61.3 22.5 %collective-permute-start.21 = (bf16[2,80,512]{2,1,0:T(8,128)(2,1)S(1)}, bf16[2,80,512]{2,1,0:T(8,128)(2,1)S(1)}, u32[]{:S(2)}, u32[]{:S(2)}) collective-permute-start(bf16[2,80,512]{2,1,0:T(8,128)(2,1)S(1)} %get-tuple-element.26), channel_id=1, source_target_pairs={{0,16},{4,20},{8,24},{12,28},{16,0},{20,4},{24,8},{28,12},{1,17},{... | collective-permute-start | bytes 491528 | tf_op jit(solution)/shard_map/ppermute | solution.py:16
  64.0 46.7 %collective-permute-start.7 = (bf16[1024,512]{1,0:T(8,128)(2,1)S(1)}, bf16[1024,512]{1,0:T(8,128)(2,1)S(1)}, u32[]{:S(2)}, u32[]{:S(2)}) collective-permute-start(bf16[1024,512]{1,0:T(8,128)(2,1)S(1)} %bitcast.79), channel_id=1, source_target_pairs={{0,1},{1,0},{2,3},{3,2},{4,5},{5,4},{6,7},{7,6},{8,9},{9,8},{10,11... | collective-permute-start | bytes 3145736 | tf_op jit(solution)/shard_map/ppermute | solution.py:16
  77.5 33.8 %collective-permute-start.9 = (bf16[1024,512]{1,0:T(8,128)(2,1)S(1)}, bf16[1024,512]{1,0:T(8,128)(2,1)S(1)}, u32[]{:S(2)}, u32[]{:S(2)}) collective-permute-start(bf16[1024,512]{1,0:T(8,128)(2,1)S(1)} %collective-permute-done.8.refs_2_), channel_id=1, source_target_pairs={{0,1},{1,0},{2,3},{3,2},{4,5},{5,4},{6,7},{7,6},{8,9},{9,8},{10,11... | collective-permute-start | bytes 3145736 | tf_op jit(solution)/shard_map/ppermute | solution.py:16
  79.3 30.6 %collective-permute-start.5 = (bf16[512,512]{1,0:T(8,128)(2,1)S(1)}, bf16[512,512]{1,0:T(8,128)(2,1)S(1)}, u32[]{:S(2)}, u32[]{:S(2)}) collective-permute-start(bf16[512,512]{1,0:T(8,128)(2,1)S(1)} %bitcast.81), channel_id=1, source_target_pairs={{0,2},{1,3},{2,0},{3,1},{4,6},{5,7},{6,4},{7,5},{8,10},{9,11},{10,... | collective-permute-start | bytes 1572872 | tf_op jit(solution)/shard_map/ppermute | solution.py:16
  80.8 29.6 %collective-permute-start.16 = (bf16[4,176,512]{2,1,0:T(8,128)(2,1)S(1)}, bf16[4,176,512]{2,1,0:T(8,128)(2,1)S(1)}, u32[]{:S(2)}, u32[]{:S(2)}) collective-permute-start(bf16[4,176,512]{2,1,0:T(8,128)(2,1)S(1)} %get-tuple-element.23), channel_id=1, source_target_pairs={{0,4},{4,0},{8,12},{12,8},{16,20},{20,16},{24,28},{28,24},{1,5},{5... | collective-permute-start | bytes 2162696 | tf_op jit(solution)/shard_map/ppermute | solution.py:16
  83.8 18.7 %collective-permute-start.22 = (bf16[2,80,512]{2,1,0:T(8,128)(2,1)S(1)}, bf16[2,80,512]{2,1,0:T(8,128)(2,1)S(1)}, u32[]{:S(2)}, u32[]{:S(2)}) collective-permute-start(bf16[2,80,512]{2,1,0:T(8,128)(2,1)S(1)} %get-tuple-element.27), channel_id=1, source_target_pairs={{0,24},{4,28},{8,16},{12,20},{16,8},{20,12},{24,0},{28,4},{1,25},{... | collective-permute-start | bytes 491528 | tf_op jit(solution)/shard_map/ppermute | solution.py:16
  102.5 7.4 %collective-permute-start.23 = (bf16[80,512]{1,0:T(8,128)(2,1)S(1)}, bf16[80,512]{1,0:T(8,128)(2,1)S(1)}, u32[]{:S(2)}, u32[]{:S(2)}) collective-permute-start(bf16[80,512]{1,0:T(8,128)(2,1)S(1)} %fusion.14), channel_id=1, source_target_pairs={{0,4},{4,0},{8,12},{12,8},{16,20},{20,16},{24,28},{28,24},{1,5},{5... | collective-permute-start | bytes 245768 | tf_op jit(solution)/shard_map/ppermute | solution.py:16
  109.9 5.2 %copy-start.2 = (bf16[2048,512]{1,0:T(8,128)(2,1)S(1)}, bf16[2048,512]{1,0:T(8,128)(2,1)}, u32[]{:S(2)}) copy-start(bf16[2048,512]{1,0:T(8,128)(2,1)} %refs_4_.3) | copy-start | bytes 6291460
  109.9 10.8 %collective-permute-start.4 = (bf16[512,512]{1,0:T(8,128)(2,1)S(1)}, bf16[512,512]{1,0:T(8,128)(2,1)S(1)}, u32[]{:S(2)}, u32[]{:S(2)}) collective-permute-start(bf16[512,512]{1,0:T(8,128)(2,1)S(1)} %bitcast.82), channel_id=1, source_target_pairs={{0,1},{1,0},{2,3},{3,2},{4,5},{5,4},{6,7},{7,6},{8,9},{9,8},{10,11... | collective-permute-start | bytes 1572872 | tf_op jit(solution)/shard_map/ppermute | solution.py:16
  109.9 10.8 %collective-permute-start.6 = (bf16[512,512]{1,0:T(8,128)(2,1)S(1)}, bf16[512,512]{1,0:T(8,128)(2,1)S(1)}, u32[]{:S(2)}, u32[]{:S(2)}) collective-permute-start(bf16[512,512]{1,0:T(8,128)(2,1)S(1)} %collective-permute-done.5.refs_2_), channel_id=1, source_target_pairs={{0,1},{1,0},{2,3},{3,2},{4,5},{5,4},{6,7},{7,6},{8,9},{9,8},{10,11... | collective-permute-start | bytes 1572872 | tf_op jit(solution)/shard_map/ppermute | solution.py:16
  110.6 15.2 %collective-permute-start.17 = (bf16[176,512]{1,0:T(8,128)(2,1)S(1)}, bf16[176,512]{1,0:T(8,128)(2,1)S(1)}, u32[]{:S(2)}, u32[]{:S(2)}) collective-permute-start(bf16[176,512]{1,0:T(8,128)(2,1)S(1)} %get-tuple-element.30), channel_id=1, source_target_pairs={{0,8},{4,12},{8,0},{12,4},{16,24},{20,28},{24,16},{28,20},{1,9},{5... | collective-permute-start | bytes 540680 | tf_op jit(solution)/shard_map/ppermute | solution.py:16
  110.7 16.2 %collective-permute-start.18 = (bf16[176,512]{1,0:T(8,128)(2,1)S(1)}, bf16[176,512]{1,0:T(8,128)(2,1)S(1)}, u32[]{:S(2)}, u32[]{:S(2)}) collective-permute-start(bf16[176,512]{1,0:T(8,128)(2,1)S(1)} %get-tuple-element.32), channel_id=1, source_target_pairs={{0,16},{4,20},{8,24},{12,28},{16,0},{20,4},{24,8},{28,12},{1,17},{... | collective-permute-start | bytes 540680 | tf_op jit(solution)/shard_map/ppermute | solution.py:16
  111.3 15.6 %collective-permute-start.19 = (bf16[176,512]{1,0:T(8,128)(2,1)S(1)}, bf16[176,512]{1,0:T(8,128)(2,1)S(1)}, u32[]{:S(2)}, u32[]{:S(2)}) collective-permute-start(bf16[176,512]{1,0:T(8,128)(2,1)S(1)} %get-tuple-element.31), channel_id=1, source_target_pairs={{0,24},{4,28},{8,16},{12,20},{16,8},{20,12},{24,0},{28,4},{1,25},{... | collective-permute-start | bytes 540680 | tf_op jit(solution)/shard_map/ppermute | solution.py:16
